TPU v7x, 128 devices: a whole 4x4x4 slice. The times are simulated.
128 devices in a mesh: group: 16 (over y, x), expert: 8 (over z, core).
Axes of the slice: x: 4, y: 4, z: 4, core: 2. Of those that a mesh axis runs over, the one named last changes fastest.
Arguments:
- tokens_in: bfloat16 [16384, 2048], P(('group', 'expert')), may hold values from -6 to 6
- out_grad: bfloat16 [16384, 2048], P(('group', 'expert')), may hold values from -3 to 3
- expert_ids: int32 [16384, 8], P(('group', 'expert')), may hold values from 0 to 127, as said below
- gate_weights: float32 [16384, 8], P(('group', 'expert')), may hold values from 0.05 to 1
- w_gate: bfloat16 [128, 2048, 768], P(('group', 'expert')), may hold values from -0.125 to 0.125
- w_up: bfloat16 [128, 2048, 768], P(('group', 'expert')), may hold values from -0.125 to 0.125
- w_down: bfloat16 [128, 768, 2048], P(('group', 'expert')), may hold values from -0.21875 to 0.21875
Outputs:
- grad_in: bfloat16 [16384, 2048], P(('group', 'expert'))
- grad_gate: bfloat16 [128, 2048, 768], P(('group', 'expert'))
- grad_up: bfloat16 [128, 2048, 768], P(('group', 'expert'))
- grad_down: bfloat16 [128, 768, 2048], P(('group', 'expert'))
Inputs may be any that keep to these rules, and one draw needn't show every extreme that they name: `expert_ids`: each row names 8 different experts. Among the 128 tokens of one device no expert is named more than 16 times, and some expert is named exactly 16 times by the tokens of some device. The tokens of one device name the experts of each group (experts g * 8 to g * 8 + 7) exactly 64 times. Over all 16384 tokens every expert is named exactly 128 * 8 times.
All inputs are finite; a program needn't handle non-finite values.
Results may differ from a plain program's by a relative error of at most 0.0065.
Values may be sent and summed in bfloat16 or wider, within the bound.
A program may use at most 128 MiB of HBM per device.

v0:
```python
import jax
import jax.numpy as jnp
from jax import lax
from jax.sharding import PartitionSpec as P


def contract_rows(first_op, second_op):
    return lax.dot_general(
        first_op, second_op, (((0,), (0,)), ((), ())), preferred_element_type=jnp.float32
    )


def contract_cols(first_op, second_op):
    return lax.dot_general(
        first_op, second_op, (((1,), (1,)), ((), ())), preferred_element_type=jnp.float32
    )


def expert_backward(inputs, grad_rows, gate_mat, up_mat, down_mat):
    gate_pre = jnp.dot(inputs, gate_mat, preferred_element_type=jnp.float32)
    up_pre = jnp.dot(inputs, up_mat, preferred_element_type=jnp.float32)
    sigma_gate = jax.nn.sigmoid(gate_pre)
    activated = gate_pre * sigma_gate
    hidden = (activated * up_pre).astype(jnp.bfloat16)
    hidden_grad = contract_cols(grad_rows, down_mat)
    down_grad = contract_rows(hidden, grad_rows).astype(jnp.bfloat16)
    gate_grad_rows = (
        hidden_grad * up_pre * sigma_gate * (1.0 + gate_pre * (1.0 - sigma_gate))
    ).astype(jnp.bfloat16)
    up_grad_rows = (hidden_grad * activated).astype(jnp.bfloat16)
    input_rows = (
        contract_cols(gate_grad_rows, gate_mat) + contract_cols(up_grad_rows, up_mat)
    ).astype(jnp.bfloat16)
    gate_weight_grad = contract_rows(inputs, gate_grad_rows).astype(jnp.bfloat16)
    up_weight_grad = contract_rows(inputs, up_grad_rows).astype(jnp.bfloat16)
    return (gate_weight_grad, up_weight_grad, down_grad, input_rows)


def body(tokens_in, out_grad, expert_ids, gate_weights, w_gate, w_up, w_down):
    groups = lax.axis_size("group")
    owners = lax.axis_size("expert")
    experts = groups * owners
    token_count, top_count = expert_ids.shape
    model_width = tokens_in.shape[1]
    assigned = token_count * top_count
    capacity = 2 * assigned // experts
    flat_ids = expert_ids.reshape(assigned)
    columns = jnp.arange(experts, dtype=jnp.int32)
    counts = jnp.sum((flat_ids[:, None] == columns[None, :]).astype(jnp.int32), axis=0)
    starts = jnp.cumsum(counts) - counts
    sorted_rows = jnp.argsort(flat_ids, stable=True)
    gate_flat = gate_weights.reshape(assigned)
    sender_pos = jnp.arange(experts, dtype=jnp.int32)
    token_cols = jnp.arange(token_count, dtype=jnp.int32)
    slot_pos = jnp.arange(experts * capacity, dtype=jnp.int32)
    slot_owner = slot_pos // capacity
    slot_index = slot_pos % capacity
    filled = slot_index < counts[slot_owner]
    source = sorted_rows[jnp.minimum(starts[slot_owner] + slot_index, assigned - 1)]
    slot_token = jnp.where(filled, source // top_count, -1)
    slot_select = (slot_token[:, None] == token_cols[None, :]).astype(jnp.bfloat16)
    rows_in = jnp.dot(slot_select, tokens_in, preferred_element_type=jnp.float32).astype(
        jnp.bfloat16
    )
    picked_grad = jnp.dot(slot_select, out_grad, preferred_element_type=jnp.float32)
    rows_grad = (gate_flat[source][:, None] * picked_grad).astype(jnp.bfloat16)
    recv_in, recv_grad, recv_counts = (
        lax.all_to_all(
            rows_in.reshape(experts, capacity, model_width),
            ("group", "expert"),
            split_axis=0,
            concat_axis=0,
            tiled=True,
        ),
        lax.all_to_all(
            rows_grad.reshape(experts, capacity, model_width),
            ("group", "expert"),
            split_axis=0,
            concat_axis=0,
            tiled=True,
        ),
        lax.all_to_all(counts, ("group", "expert"), split_axis=0, concat_axis=0, tiled=True),
    )
    sender_base = sender_pos * capacity
    recv_in = recv_in.reshape(experts * capacity, model_width)
    recv_grad = recv_grad.reshape(experts * capacity, model_width)
    recv_ends = jnp.cumsum(recv_counts)
    recv_starts = recv_ends - recv_counts
    live_rows = jnp.arange(assigned, dtype=jnp.int32)
    sender = jnp.minimum(
        jnp.sum((live_rows[:, None] >= recv_ends[None, :]).astype(jnp.int32), axis=1), experts - 1
    )
    gather_rows = sender_base[sender] + live_rows - recv_starts[sender]
    inputs = recv_in[gather_rows]
    grad_rows = recv_grad[gather_rows]
    gate_weight_grad, up_weight_grad, down_grad, input_rows = expert_backward(
        inputs, grad_rows, w_gate[0], w_up[0], w_down[0]
    )
    back_slot = jnp.arange(experts * capacity, dtype=jnp.int32)
    back_off = back_slot % capacity
    back_sender = back_slot // capacity
    kept = back_off < recv_counts[back_sender]
    back_pos = jnp.minimum(recv_starts[back_sender] + back_off, assigned - 1)
    returned = jnp.where(kept[:, None], input_rows[back_pos], 0)
    arrived = lax.all_to_all(
        returned.reshape(experts, capacity, model_width),
        ("group", "expert"),
        split_axis=0,
        concat_axis=0,
        tiled=True,
    )
    arrived = arrived.reshape(experts * capacity, model_width)
    summed = contract_rows(slot_select, arrived)
    grad_in = summed.astype(jnp.bfloat16)
    return (grad_in, gate_weight_grad[None], up_weight_grad[None], down_grad[None])


def solution(mesh):
    return jax.shard_map(
        body,
        mesh=mesh,
        in_specs=(
            P(("group", "expert"), None),
            P(("group", "expert"), None),
            P(("group", "expert"), None),
            P(("group", "expert"), None),
            P(("group", "expert"), None, None),
            P(("group", "expert"), None, None),
            P(("group", "expert"), None, None),
        ),
        out_specs=(
            P(("group", "expert"), None),
            P(("group", "expert"), None, None),
            P(("group", "expert"), None, None),
            P(("group", "expert"), None, None),
        ),
        check_vma=False,
    )
```

profile of v0, /device:TPU:9, one launch (start us, length us, event | category | flops | bytes accessed | tf_op | source)
XLA Modules:
  0.0 473.1 jit_solution(1006947215242302310)
XLA Ops:
  2.6 10.7 %all-to-all-start = ((s32[128,1,1]{2,1,0:T(1,128)}), s32[128,1,1]{2,1,0:T(1,128)S(1)}, u32[]{:S(2)}, u32[]{:S(2)}) async-start(s32[128,1,1]{2,1,0:T(1,128)} %copy.29), calls=%async_computation | async-start | bytes 131072 | tf_op jit(solution)/shard_map/all_to_all | solution.py:82
  13.4 4.4 sort.17
  17.8 12.6 %gather_fusion = s32[2048]{0:T(1024)S(1)} fusion(s32[128]{0:T(128)S(1)} %convert_reduce_fusion.1, s32[2048]{0:T(1024)S(1)} %broadcast_clamp_fusion.3), kind=kCustom, calls=%fused_computation | custom fusion | bytes 24576 | tf_op jit(solution)/shard_map/gather | solution.py:58
  30.8 12.6 %gather_fusion.1 = s32[2048]{0:T(1024)S(1)} fusion(s32[128]{0:T(128)S(1)} %sub.38, s32[2048]{0:T(1024)S(1)} %broadcast_clamp_fusion.3), kind=kCustom, calls=%fused_computation.1 | custom fusion | bytes 24576 | tf_op jit(solution)/shard_map/gather | solution.py:59
  43.5 8.6 %gather_fusion.2 = s32[2048]{0:T(1024)S(1)} fusion(s32[1024]{0:T(1024)S(1)} %get-tuple-element.5, s32[2048]{0:T(1024)S(1)} %broadcast_clamp_fusion.2), kind=kCustom, calls=%fused_computation.2 | custom fusion | bytes 24576 | tf_op jit(solution)/shard_map/gather | solution.py:59
  52.3 8.6 %gather_fusion.4 = f32[2048]{0:T(1024)S(1)} fusion(f32[1024]{0:T(1024)S(1)} %reshape.274, s32[2048]{0:T(1024)S(1)} %broadcast_clamp_fusion.1), kind=kCustom, calls=%fused_computation.4 | custom fusion | bytes 24576 | tf_op jit(solution)/shard_map/gather | solution.py:66
  60.9 5.6 %multiply_convert_fusion = bf16[2048,2048]{1,0:T(8,128)(2,1)} fusion(bf16[128,2048]{1,0:T(8,128)(2,1)} %param.8, f32[2048]{0:T(1024)S(1)} %gather_fusion.4, s32[2048]{0:T(1024)S(1)} %fusion.23), kind=kOutput, calls=%fused_computation.11 | convolution fusion | flops 1082392576 | bytes 8929280 | tf_op jit(solution)/shard_map/dot_general | solution.py:65
  66.5 10.2 %all-to-all-start.1 = ((bf16[128,16,2048]{2,1,0:T(8,128)(2,1)}), bf16[128,16,2048]{2,1,0:T(8,128)(2,1)}, u32[]{:S(2)}, u32[]{:S(2)}) async-start(bf16[128,16,2048]{2,1,0:T(8,128)(2,1)} %bitcast.58), calls=%async_computation.1 | async-start | bytes 16777216 | tf_op jit(solution)/shard_map/all_to_all | solution.py:75
  76.8 5.6 %convolution_convert_fusion = bf16[2048,2048]{1,0:T(8,128)(2,1)} fusion(bf16[128,2048]{1,0:T(8,128)(2,1)} %param.7, s32[2048]{0:T(1024)S(1)} %fusion.23), kind=kOutput, calls=%fused_computation.14 | convolution fusion | flops 1078198272 | bytes 8921088 | tf_op jit(solution)/shard_map/dot_general | solution.py:62
  82.4 95.3 %all-to-all-done.1 = bf16[128,16,2048]{2,1,0:T(8,128)(2,1)} async-done(((bf16[128,16,2048]{2,1,0:T(8,128)(2,1)}), bf16[128,16,2048]{2,1,0:T(8,128)(2,1)}, u32[]{:S(2)}, u32[]{:S(2)}) %all-to-all-start.1) | async-done | bytes 8388640 | tf_op jit(solution)/shard_map/all_to_all | solution.py:75
  177.7 12.5 %all-to-all-start.2 = ((bf16[128,16,2048]{2,1,0:T(8,128)(2,1)}), bf16[128,16,2048]{2,1,0:T(8,128)(2,1)}, u32[]{:S(2)}, u32[]{:S(2)}) async-start(bf16[128,16,2048]{2,1,0:T(8,128)(2,1)} %bitcast.57), calls=%async_computation.2 | async-start | bytes 16777216 | tf_op jit(solution)/shard_map/all_to_all | solution.py:68
  190.5 2.4 reduce.1
  192.8 12.6 %gather_fusion.3 = s32[2048]{0:T(1024)S(1)} fusion(s32[128]{0:T(128)S(1)} %reduce.1, s32[2048]{0:T(1024)S(1)} %broadcast_clamp_fusion.3), kind=kCustom, calls=%fused_computation.3 | custom fusion | bytes 24576 | tf_op jit(solution)/shard_map/gather | solution.py:102
  205.4 12.6 %gather_fusion.9 = s32[2048]{0:T(1024)S(1)} fusion(s32[128]{0:T(128)S(1)} %sub.40, s32[2048]{0:T(1024)S(1)} %broadcast_clamp_fusion.3), kind=kCustom, calls=%fused_computation.9 | custom fusion | bytes 24576 | tf_op jit(solution)/shard_map/gather | solution.py:103
  218.3 6.6 %gather_fusion.6 = s32[1024]{0:T(1024)S(1)} fusion(s32[128]{0:T(128)S(1)} %sub.40, s32[1024]{0:T(1024)S(1)} %broadcast_clamp_fusion.5), kind=kCustom, calls=%fused_computation.6 | custom fusion | bytes 12288 | tf_op jit(solution)/shard_map/gather | solution.py:93
  224.9 6.6 %gather_fusion.5 = s32[1024]{0:T(1024)S(1)} fusion(s32[128]{0:T(128)S(1)} %iota_multiply_fusion, s32[1024]{0:T(1024)S(1)} %broadcast_clamp_fusion.5), kind=kCustom, calls=%fused_computation.5 | custom fusion | bytes 12288 | tf_op jit(solution)/shard_map/gather | solution.py:93
  231.7 13.3 %gather_fusion.7 = bf16[1024,2048]{1,0:T(8,128)(2,1)} fusion(bf16[2048,2048]{1,0:T(8,128)(2,1)} %bitcast.8, s32[1024]{0:T(1024)S(1)} %broadcast_clamp_fusion.4), kind=kCustom, calls=%fused_computation.7 | custom fusion | bytes 8392704 | tf_op jit(solution)/shard_map/gather | solution.py:95
  245.0 45.4 %all-to-all-done.2 = bf16[128,16,2048]{2,1,0:T(8,128)(2,1)} async-done(((bf16[128,16,2048]{2,1,0:T(8,128)(2,1)}), bf16[128,16,2048]{2,1,0:T(8,128)(2,1)}, u32[]{:S(2)}, u32[]{:S(2)}) %all-to-all-start.2) | async-done | bytes 8388640 | tf_op jit(solution)/shard_map/all_to_all | solution.py:68
  290.4 13.3 %gather_fusion.8 = bf16[1024,2048]{1,0:T(8,128)(2,1)} fusion(bf16[2048,2048]{1,0:T(8,128)(2,1)} %bitcast.17, s32[1024]{0:T(1024)S(1)} %broadcast_clamp_fusion.4), kind=kCustom, calls=%fused_computation.8 | custom fusion | bytes 8392704 | tf_op jit(solution)/shard_map/gather | solution.py:94
  303.7 5.6 %fusion.2 = f32[1024,768]{1,0:T(8,128)S(1)} fusion(bf16[1024,2048]{1,0:T(8,128)(2,1)} %gather_fusion.8, bf16[1,2048,768]{2,1,0:T(8,128)(2,1)S(1)} %copy-done), kind=kOutput, calls=%fused_computation.20 | convolution fusion | flops 3221225472 | bytes 10485760 | tf_op jit(solution)/shard_map/dot_general | solution.py:20
  309.4 3.4 fusion.5
  313.7 4.3 multiply_convert_fusion.2
  318.0 3.5 fusion
  321.5 5.0 %add_convert_fusion = bf16[1024,2048]{1,0:T(8,128)(2,1)} fusion(f32[1024,2048]{1,0:T(8,128)S(1)} %fusion, bf16[1024,768]{1,0:T(8,128)(2,1)S(1)} %get-tuple-element.6, bf16[1,2048,768]{2,1,0:T(8,128)(2,1)S(1)} %copy-done.8), kind=kOutput, calls=%fused_computation.12 | convolution fusion | flops 3225419776 | bytes 17301504 | tf_op jit(solution)/shard_map/dot_general | solution.py:14
  326.5 19.1 %gather_fusion.10 = bf16[2048,2048]{1,0:T(8,128)(2,1)} fusion(bf16[1024,2048]{1,0:T(8,128)(2,1)} %add_convert_fusion, s32[2048]{0:T(1024)S(1)} %broadcast_clamp_fusion), kind=kCustom, calls=%fused_computation.10 | custom fusion | bytes 16785408 | tf_op jit(solution)/shard_map/gather | solution.py:104
  345.6 7.4 %broadcast_select_fusion = bf16[128,16,2048]{2,1,0:T(8,128)(2,1)} fusion(bf16[128,16,2048]{2,1,0:T(8,128)(2,1)} %bitcast.59, pred[128,16]{1,0:T(8,128)(4,1)S(1)} %fusion.17), kind=kLoop, calls=%fused_computation.13 | loop fusion | flops 4194304 | bytes 16779264 | tf_op jit(solution)/shard_map/jit(_where)/select_n | solution.py:104
  353.0 13.0 %all-to-all-start.3 = ((bf16[128,16,2048]{2,1,0:T(8,128)(2,1)}), bf16[128,16,2048]{2,1,0:T(8,128)(2,1)}, u32[]{:S(2)}, u32[]{:S(2)}) async-start(bf16[128,16,2048]{2,1,0:T(8,128)(2,1)} %broadcast_select_fusion), calls=%async_computation.3 | async-start | bytes 16777216 | tf_op jit(solution)/shard_map/all_to_all | solution.py:105
  366.0 7.5 %fusion.11 = bf16[1,2048,768]{2,1,0:T(8,128)(2,1)} fusion(bf16[1024,2048]{1,0:T(8,128)(2,1)} %gather_fusion.8, bf16[1024,768]{1,0:T(8,128)(2,1)S(1)} %copy-done.16), kind=kOutput, calls=%fused_computation.33 | convolution fusion | flops 3222798336 | bytes 8912896 | tf_op jit(solution)/shard_map/dot_general | solution.py:8
  373.6 4.9 %fusion.10 = bf16[1,2048,768]{2,1,0:T(8,128)(2,1)} fusion(bf16[1024,2048]{1,0:T(8,128)(2,1)S(1)} %copy-done.5, bf16[1024,768]{1,0:T(8,128)(2,1)S(1)} %copy-done.14), kind=kOutput, calls=%fused_computation.32 | convolution fusion | flops 3222798336 | bytes 8912896 | tf_op jit(solution)/shard_map/dot_general | solution.py:8
  378.5 5.2 %fusion.12 = bf16[1,768,2048]{2,1,0:T(8,128)(2,1)} fusion(bf16[1024,2048]{1,0:T(8,128)(2,1)S(1)} %copy-done.3, f32[1024,768]{1,0:T(8,128)S(1)} %copy-done.12, f32[1024,768]{1,0:T(8,128)S(1)} %copy-done.10), kind=kOutput, calls=%fused_computation.34 | convolution fusion | flops 3227516928 | bytes 13631488 | tf_op jit(solution)/shard_map/dot_general | solution.py:8
  383.7 83.2 %all-to-all-done.3 = bf16[128,16,2048]{2,1,0:T(8,128)(2,1)} async-done(((bf16[128,16,2048]{2,1,0:T(8,128)(2,1)}), bf16[128,16,2048]{2,1,0:T(8,128)(2,1)}, u32[]{:S(2)}, u32[]{:S(2)}) %all-to-all-start.3) | async-done | bytes 8388640 | tf_op jit(solution)/shard_map/all_to_all | solution.py:105
  466.9 5.8 %convolution_convert_fusion.4 = bf16[128,2048]{1,0:T(8,128)(2,1)} fusion(bf16[2048,2048]{1,0:T(8,128)(2,1)} %bitcast.23, s32[2048]{0:T(1024)S(1)} %fusion.23), kind=kOutput, calls=%fused_computation.35 | convolution fusion | flops 1074266112 | bytes 8921088 | tf_op jit(solution)/shard_map/dot_general | solution.py:8
  (67 shorter events, 4.2 us)
Async XLA Ops:
  0.6 303.1 %copy-start = (bf16[1,2048,768]{2,1,0:T(8,128)(2,1)S(1)}, bf16[1,2048,768]{2,1,0:T(8,128)(2,1)}, u32[]{:S(2)}) copy-start(bf16[1,2048,768]{2,1,0:T(8,128)(2,1)} %param.11) | copy-start | bytes 9437188
  2.6 63.9 %all-to-all-start = ((s32[128,1,1]{2,1,0:T(1,128)}), s32[128,1,1]{2,1,0:T(1,128)S(1)}, u32[]{:S(2)}, u32[]{:S(2)}) async-start(s32[128,1,1]{2,1,0:T(1,128)} %copy.29), calls=%async_computation | async-start | bytes 131072 | tf_op jit(solution)/shard_map/all_to_all | solution.py:82
  43.5 8.7 %copy-start.6 = (f32[128,8]{0,1:T(8,128)S(1)}, f32[128,8]{0,1:T(8,128)}, u32[]{:S(2)}) copy-start(f32[128,8]{0,1:T(8,128)} %param.10) | copy-start | bytes 12292
  66.5 111.1 %all-to-all-start.1 = ((bf16[128,16,2048]{2,1,0:T(8,128)(2,1)}), bf16[128,16,2048]{2,1,0:T(8,128)(2,1)}, u32[]{:S(2)}, u32[]{:S(2)}) async-start(bf16[128,16,2048]{2,1,0:T(8,128)(2,1)} %bitcast.58), calls=%async_computation.1 | async-start | bytes 16777216 | tf_op jit(solution)/shard_map/all_to_all | solution.py:75
  177.7 112.7 %all-to-all-start.2 = ((bf16[128,16,2048]{2,1,0:T(8,128)(2,1)}), bf16[128,16,2048]{2,1,0:T(8,128)(2,1)}, u32[]{:S(2)}, u32[]{:S(2)}) async-start(bf16[128,16,2048]{2,1,0:T(8,128)(2,1)} %bitcast.57), calls=%async_computation.2 | async-start | bytes 16777216 | tf_op jit(solution)/shard_map/all_to_all | solution.py:68
  303.7 5.6 %copy-start.4 = (bf16[1024,2048]{1,0:T(8,128)(2,1)S(1)}, bf16[1024,2048]{1,0:T(8,128)(2,1)}, u32[]{:S(2)}) copy-start(bf16[1024,2048]{1,0:T(8,128)(2,1)} %gather_fusion.8) | copy-start | bytes 12582916
  303.7 5.7 %copy-start.8 = (bf16[1,2048,768]{2,1,0:T(8,128)(2,1)S(1)}, bf16[1,2048,768]{2,1,0:T(8,128)(2,1)}, u32[]{:S(2)}) copy-start(bf16[1,2048,768]{2,1,0:T(8,128)(2,1)} %param.12) | copy-start | bytes 9437188
  309.4 3.5 copy-start.9
  309.4 3.5 copy-start.2
  309.4 4.3 copy-start.7
  313.7 4.3 copy-start.11
  318.0 3.5 copy-start.13
  318.0 3.5 copy-start.15
  353.0 13.0 %copy-start.16 = (bf16[1024,768]{1,0:T(8,128)(2,1)S(1)}, bf16[1024,768]{1,0:T(8,128)(2,1)}, u32[]{:S(2)}) copy-start(bf16[1024,768]{1,0:T(8,128)(2,1)} %copy-done.15) | copy-start | bytes 4718596
  353.0 113.9 %all-to-all-start.3 = ((bf16[128,16,2048]{2,1,0:T(8,128)(2,1)}), bf16[128,16,2048]{2,1,0:T(8,128)(2,1)}, u32[]{:S(2)}, u32[]{:S(2)}) async-start(bf16[128,16,2048]{2,1,0:T(8,128)(2,1)} %broadcast_select_fusion), calls=%async_computation.3 | async-start | bytes 16777216 | tf_op jit(solution)/shard_map/all_to_all | solution.py:105
  366.0 7.6 %copy-start.5 = (bf16[1024,2048]{1,0:T(8,128)(2,1)S(1)}, bf16[1024,2048]{1,0:T(8,128)(2,1)}, u32[]{:S(2)}) copy-start(bf16[1024,2048]{1,0:T(8,128)(2,1)} %gather_fusion.8) | copy-start | bytes 12582916
  366.0 7.6 %copy-start.14 = (bf16[1024,768]{1,0:T(8,128)(2,1)S(1)}, bf16[1024,768]{1,0:T(8,128)(2,1)}, u32[]{:S(2)}) copy-start(bf16[1024,768]{1,0:T(8,128)(2,1)} %copy-done.13) | copy-start | bytes 4718596
  373.6 4.9 %copy-start.3 = (bf16[1024,2048]{1,0:T(8,128)(2,1)S(1)}, bf16[1024,2048]{1,0:T(8,128)(2,1)}, u32[]{:S(2)}) copy-start(bf16[1024,2048]{1,0:T(8,128)(2,1)} %gather_fusion.7) | copy-start | bytes 12582916
  373.6 4.9 %copy-start.10 = (f32[1024,768]{1,0:T(8,128)S(1)}, f32[1024,768]{1,0:T(8,128)}, u32[]{:S(2)}) copy-start(f32[1024,768]{1,0:T(8,128)} %copy-done.9) | copy-start | bytes 9437188
  373.6 4.9 %copy-start.12 = (f32[1024,768]{1,0:T(8,128)S(1)}, f32[1024,768]{1,0:T(8,128)}, u32[]{:S(2)}) copy-start(f32[1024,768]{1,0:T(8,128)} %copy-done.11) | copy-start | bytes 9437188
  466.9 5.8 %copy-start.1 = (bf16[1,2048,768]{2,1,0:T(8,128)(2,1)S(1)}, bf16[1,2048,768]{2,1,0:T(8,128)(2,1)}, u32[]{:S(2)}) copy-start(bf16[1,2048,768]{2,1,0:T(8,128)(2,1)} %param.11) | copy-start | bytes 9437188
where the time goes:
time: 482 us; the launch traced here: 473 us
  waiting for transfers between devices  224 us (46%)
  local copies, waits for them, and re-layouts  129 us (27%)
  matrix products  56.5 us (12%)
  starting transfers between devices  46.4 us (10%)
  other arithmetic  15.3 us (3%)
    all_to_all x1, waiting for transfers between devices, body(): lax.all_to_all(rows_grad.reshape(experts, capacity, model_width), ('group...  95.3 us
    all_to_all x1, waiting for transfers between devices, body(): lax.all_to_all(returned.reshape(experts, capacity, model_width), ('group'...  83.2 us
    all_to_all x1, waiting for transfers between devices, body(): lax.all_to_all(rows_in.reshape(experts, capacity, model_width), ('group',...  45.4 us
    dot_general x4, matrix products, contract_rows(): lax.dot_general(first_op, second_op, (((0,), (0,)), ((), ())), preferred_...  23.4 us
    gather x1, local copies, waits for them, and re-layouts, body(): returned = jnp.where(kept[:, None], input_rows[back_pos], 0)  19.1 us
    gather x1, local copies, waits for them, and re-layouts, body(): grad_rows = recv_grad[gather_rows]  13.3 us
    gather x1, local copies, waits for them, and re-layouts, body(): inputs = recv_in[gather_rows]  13.3 us
    gather x2, local copies, waits for them, and re-layouts, body(): gather_rows = sender_base[sender] + live_rows - recv_starts[sender]  13.1 us
  transfers between devices with their start and end apart: 4, of which 3 were waited for; matrix products, arithmetic and copies ran while one was open for 28% of the time, Pallas kernels for 0%

commit v1 on v0

v1 whole, which is shorter than its diff:
```python
import jax
import jax.numpy as jnp
from jax import lax
from jax.experimental import pallas as pl
from jax.experimental.pallas import tpu as pltpu
from jax.sharding import PartitionSpec as P

NG, NJ = 16, 8
T, D, FF = 128, 2048, 768
CAP = 16
PG = 64
E = NG * NJ
ROWS = NG * NJ * CAP
BF, F32, I32 = jnp.bfloat16, jnp.float32, jnp.int32
MESH = pl.DeviceIdType.MESH
VMEM_LIMIT = 67043328


def dot(a, b, ca=1, cb=0):
    return lax.dot_general(a, b, (((ca,), (cb,)), ((), ())), preferred_element_type=F32)


def shift_of(d):
    if isinstance(d, int):
        return d % 4, (d // 4 + d % 4) % 4
    dy = lax.rem(d, 4)
    return dy, lax.rem(lax.div(d, 4) + dy, 4)


def group_to(grp, d):
    dy, dx = shift_of(d)
    return lax.rem(lax.div(grp, 4) + dy, 4) * 4 + lax.rem(lax.rem(grp, 4) + dx, 4)


def group_from(grp, d):
    dy, dx = shift_of(d)
    return lax.rem(lax.div(grp, 4) - dy + 4, 4) * 4 + lax.rem(lax.rem(grp, 4) - dx + 4, 4)


def enter(grp, own):
    barrier = pltpu.get_barrier_semaphore()
    for d in range(1, NG):
        pl.semaphore_signal(barrier, inc=1, device_id=(group_to(grp, d), own), device_id_type=MESH)
    for k in range(1, NJ):
        pl.semaphore_signal(
            barrier, inc=1, device_id=(grp, lax.rem(own + k, NJ)), device_id_type=MESH
        )
    return barrier


def send(src, dst, ssem, rsem, device):
    pltpu.make_async_remote_copy(
        src_ref=src, dst_ref=dst, send_sem=ssem, recv_sem=rsem,
        device_id=device, device_id_type=MESH,
    ).start()


def landed(ref, sem):
    pltpu.make_async_copy(ref, ref, sem).wait()


def iota(shape, dim):
    return lax.broadcasted_iota(I32, shape, dim)


def dispatch_kernel(
    ids_ref, gw_ref, x_hbm, g_ref, wg_hbm, wu_hbm, wd_hbm,
    xr, gr, hid_o, gg_o, ug_o, c_o, pos_o,
    ax, pbuf, s1, r1, s2, stx, stg, wg, wu, wd, ost,
    rank_s, rank_r, pos_s, pos_r, post, wt,
    axs, axr, ms, mr, ps, pr, q1s, q1r, q2s, q2r, p2s, p2r, wsem, xsem, gsem, osem,
):
    grp, own = lax.axis_index("group"), lax.axis_index("expert")
    partner = own + 1 - 2 * lax.rem(own, 2)
    barrier = enter(grp, own)
    loads = [
        pltpu.make_async_copy(wg_hbm, wg, wsem.at[0]),
        pltpu.make_async_copy(wu_hbm, wu, wsem.at[1]),
        pltpu.make_async_copy(wd_hbm, wd, wsem.at[2]),
    ]
    pltpu.make_async_copy(x_hbm, ax.at[own], axr.at[own]).start()

    row, lane = iota((E, T), 0), iota((E, T), 1)
    before = jnp.where(row < lane, 1.0, 0.0).astype(BF)
    named = jnp.zeros((E, T), F32)
    weight = jnp.zeros((E, T), F32)
    named_p = jnp.zeros((E, T), F32)
    row_p = lax.rem(row, NG) * NJ + lax.div(row, NG)
    for k in range(8):
        idk = ids_ref[k : k + 1, :]
        gwk = gw_ref[k : k + 1, :]
        named = jnp.where(row == idk, 1.0, named)
        weight = jnp.where(row == idk, gwk, weight)
        named_p = jnp.where(row_p == idk, 1.0, named_p)
    rank = dot(named.astype(BF), before)
    rank_p = dot(named_p.astype(BF), before)
    counts = dot(named.astype(BF), jnp.ones((T, T), BF))
    ahead = jnp.where(
        (lax.div(row, NJ) == lax.div(lane, NJ)) & (lane < row), 1.0, 0.0
    ).astype(BF)
    starts = dot(ahead, counts.astype(BF))
    post[...] = jnp.where(named > 0.5, starts + rank, -1.0).astype(I32)
    wt[...] = weight
    rank_s[...] = jnp.where(named_p > 0.5, rank_p, -1.0).astype(I32).reshape(NJ, NG, T)
    mine = lax.rem(row, NJ) == lax.div(lane, CAP)
    pick = jnp.where(lax.div(iota((NG, E), 1), NJ) == iota((NG, E), 0), 1.0, 0.0).astype(BF)
    start_row = dot(pick, jnp.where(mine, starts, 0.0).astype(BF))
    count_row = dot(pick, jnp.where(mine, counts, 0.0).astype(BF))
    slot = lax.rem(iota((NG, E), 1), CAP).astype(F32)
    pos = jnp.where(slot < count_row, start_row + slot, -1.0).astype(I32)
    for a in range(NG):
        pos_s[a] = jnp.broadcast_to(pos[a : a + 1, :], (8, 128))
    rank_r[own] = rank_s[own]
    pos_r[grp] = pos_s[grp]

    pl.semaphore_wait(barrier, NG + NJ - 2)

    for k in range(1, NJ):
        to = lax.rem(own + k, NJ)
        send(rank_s.at[to], rank_r.at[own], ms.at[k], mr.at[own], (grp, to))
    for i in range(1, 4):
        to = lax.rem(own + 2 * i, NJ)
        send(x_hbm, ax.at[own], axs.at[i], axr.at[own], (grp, to))
    send(x_hbm, ax.at[own], axs.at[0], axr.at[own], (grp, partner))

    spot = iota((PG, T), 0)
    for b in range(4):
        picks, scales = [], []
        for q in range(4):
            a = group_to(grp, 4 * b + q)
            at = pl.ds(pl.multiple_of(a * NJ, NJ), NJ)
            prow, wrow = post[at, :], wt[at, :]
            hot = jnp.zeros((PG, T), F32)
            wsel = jnp.zeros((PG, T), F32)
            for e in range(NJ):
                hit = spot == prow[e : e + 1, :]
                hot = jnp.where(hit, 1.0, hot)
                wsel = jnp.where(hit, wrow[e : e + 1, :], wsel)
            c_o[pl.ds(pl.multiple_of(a * PG, PG), PG), :] = hot.astype(BF)
            picks.append(hot.astype(BF))
            scales.append(jnp.sum(wsel, axis=1, keepdims=True))
        hots = jnp.concatenate(picks, axis=0)
        scale = jnp.concatenate(scales, axis=0)
        for c in range(0, D, 512):
            part = (scale * dot(hots, g_ref[:, c : c + 512])).astype(BF)
            for q in range(4):
                s1[group_to(grp, 4 * b + q), :, c : c + 512] = part[q * PG : (q + 1) * PG, :]
        for q in range(4):
            d = 4 * b + q
            if d == 0:
                continue
            a = group_to(grp, d)
            send(pos_s.at[a], pos_r.at[grp], ps.at[d], pr.at[grp], (a, own))
            send(s1.at[a], r1.at[grp], q1s.at[d], q1r.at[grp], (a, own))
    for w in loads:
        w.start()

    def spread(a, rows_ref):
        hot = jnp.where(spot == pos_r[a, 0:1, :], 1.0, 0.0).astype(BF)
        for c in range(0, D, 512):
            s2[a, :, c : c + 512] = dot(hot, rows_ref[a, :, c : c + 512], 0, 0).astype(BF)
        for k in range(1, NJ):
            to = lax.rem(own + k, NJ)
            at = pl.ds(pl.multiple_of(to * CAP, CAP), CAP)
            send(s2.at[a, at], gr.at[a, own], q2s.at[a], q2r.at[a], (grp, to))
        at = pl.ds(pl.multiple_of(own * CAP, CAP), CAP)
        pltpu.make_async_copy(s2.at[a, at], gr.at[a, own], q2r.at[a]).start()

    spread(grp, s1)

    for i in range(1, 4):
        slot_i = lax.rem(own - 2 * i + NJ, NJ)
        landed(ax.at[slot_i], axr.at[slot_i])
        send(ax.at[slot_i], ax.at[slot_i], axs.at[3 + i], axr.at[slot_i], (grp, partner))
    for i in range(4):
        slot_i = lax.rem(partner + 2 * i, NJ)
        landed(ax.at[slot_i], axr.at[slot_i])
    landed(ax.at[own], axr.at[own])
    for k in range(1, NJ):
        frm = lax.rem(own + k, NJ)
        landed(rank_r.at[frm], mr.at[frm])

    cap_row = iota((CAP, T), 0)

    @pl.loop(0, NJ)
    def _(j):
        hots = jnp.concatenate(
            [
                jnp.where(cap_row == rank_r[j, a : a + 1, :], 1.0, 0.0).astype(BF)
                for a in range(NG)
            ],
            axis=0,
        )
        for c in range(0, D, 512):
            part = dot(hots, ax[j, :, c : c + 512]).astype(BF)
            pbuf[:, j, :, c : c + 512] = part.reshape(NG, CAP, 512)

    for d in range(1, NG):
        a = group_to(grp, d)
        send(pbuf.at[a], xr.at[grp], p2s.at[d], p2r.at[grp], (a, own))
    pltpu.make_async_copy(pbuf.at[grp], xr.at[grp], p2r.at[grp]).start()

    @pl.loop(1, NG)
    def _(d):
        a = group_from(grp, d)
        landed(pos_r.at[a], pr.at[a])
        landed(r1.at[a], q1r.at[a])
        spread(a, r1)

    for w in loads:
        w.wait()

    def fetch(i, s):
        for h in range(2):
            a = group_from(grp, 2 * i + h)
            landed(xr.at[a], p2r.at[a])
            landed(gr.at[a], q2r.at[a])
            pltpu.make_async_copy(xr.at[a], stx.at[s, pl.ds(h * NJ, NJ)], xsem.at[s]).start()
            pltpu.make_async_copy(gr.at[a], stg.at[s, pl.ds(h * NJ, NJ)], gsem.at[s]).start()

    fetch(0, 0)

    @pl.loop(0, NG // 2)
    def _(i):
        s = lax.rem(i, 2)

        @pl.when(i >= 2)
        def _():
            landed(ost.at[s], osem.at[s])

        @pl.when(i + 1 < NG // 2)
        def _():
            fetch(i + 1, 1 - s)

        landed(stx.at[s], xsem.at[s])
        landed(stg.at[s], gsem.at[s])
        xb = stx[s].reshape(2 * T, D)
        gb = stg[s].reshape(2 * T, D)
        gate_pre = dot(xb, wg[...])
        up_pre = dot(xb, wu[...])
        hgrad = dot(gb, wd[...], 1, 1)
        sigma = jax.nn.sigmoid(gate_pre)
        act = gate_pre * sigma
        hid = (act * up_pre).astype(BF)
        gg = (hgrad * up_pre * sigma * (1.0 + gate_pre * (1.0 - sigma))).astype(BF)
        ug = (hgrad * act).astype(BF)
        for h in range(2):
            a = group_from(grp, 2 * i + h)
            for n, (val, out) in enumerate(((hid, hid_o), (gg, gg_o), (ug, ug_o))):
                ost[s, h, n] = val[h * T : (h + 1) * T, :]
                pltpu.make_async_copy(ost.at[s, h, n], out.at[a], osem.at[s]).start()

    pos_o[...] = pos_r[...]
    for s in range(2):
        landed(ost.at[s], osem.at[s])
    for k in range(1, NJ):
        to = lax.rem(own + k, NJ)
        landed(rank_s.at[to], ms.at[k])
    for i in range(7):
        landed(x_hbm, axs.at[i])
    for d in range(1, NG):
        a = group_to(grp, d)
        landed(pos_s.at[a], ps.at[d])
        landed(s1.at[a], q1s.at[d])
        landed(pbuf.at[a], p2s.at[d])
    for a in range(NG):
        landed(s2.at[a, pl.ds(0, (NJ - 1) * CAP)], q2s.at[a])


def combine_kernel(
    c_ref, pos_ref, xr, gr, hid_hbm, gg_hbm, ug_hbm, wg_hbm, wu_hbm,
    gin_o, dg_o, du_o, dd_o,
    hid, gg, ug, wg, wu, dx, rr1, s2, rr2, xcol, gcol, ogu, od,
    lsem, t1s, t1r, t2s, t2r, xsem, gsem, gusem, dsem,
):
    grp, own = lax.axis_index("group"), lax.axis_index("expert")
    barrier = enter(grp, own)
    loads = [
        pltpu.make_async_copy(src, dst, lsem.at[n])
        for n, (src, dst) in enumerate(
            ((gg_hbm, gg), (ug_hbm, ug), (wg_hbm, wg), (wu_hbm, wu), (hid_hbm, hid))
        )
    ]
    for w in loads:
        w.start()
    for w in loads[:4]:
        w.wait()
    pl.semaphore_wait(barrier, NG + NJ - 2)

    @pl.loop(0, NG // 2)
    def _(i):
        tops = [group_to(grp, 2 * i + h) for h in range(2)]
        ggb = jnp.concatenate([gg[a] for a in tops], axis=0)
        ugb = jnp.concatenate([ug[a] for a in tops], axis=0)
        for c in range(0, D, 512):
            part = dot(ggb, wg[c : c + 512, :], 1, 1) + dot(ugb, wu[c : c + 512, :], 1, 1)
            part = part.astype(BF)
            for h in range(2):
                dx[tops[h], :, c : c + 512] = part[h * T : (h + 1) * T, :]
        for a in tops:
            for k in range(1, NJ):
                to = lax.rem(own + k, NJ)
                at = pl.ds(pl.multiple_of(to * CAP, CAP), CAP)
                back = pl.ds(pl.multiple_of(own * CAP, CAP), CAP)
                send(dx.at[a, at], rr1.at[a, back], t1s.at[a], t1r.at[a], (grp, to))
            at = pl.ds(pl.multiple_of(own * CAP, CAP), CAP)
            pltpu.make_async_copy(dx.at[a, at], rr1.at[a, at], t1r.at[a]).start()

    loads[4].wait()
    spot = iota((PG, T), 0)

    def fetch(c, s):
        at = pl.ds(pl.multiple_of(c * 256, 256), 256)
        pltpu.make_async_copy(xr.at[:, at], xcol.at[s], xsem.at[s]).start()
        pltpu.make_async_copy(gr.at[:, at], gcol.at[s], gsem.at[s]).start()

    fetch(0, 0)

    @pl.loop(0, NG // 2)
    def _(i):
        s = lax.rem(i, 2)

        @pl.when(i >= 2)
        def _():
            landed(ogu.at[s], gusem.at[s])
            landed(od.at[s], dsem.at[s])

        @pl.when(i + 1 < NG // 2)
        def _():
            fetch(i + 1, 1 - s)

        landed(xcol.at[s], xsem.at[s])
        landed(gcol.at[s], gsem.at[s])
        at = pl.ds(pl.multiple_of(i * 256, 256), 256)
        xc = xcol[s]
        ogu[s, 0] = dot(xc, gg[...].reshape(ROWS, FF), 0, 0).astype(BF)
        ogu[s, 1] = dot(xc, ug[...].reshape(ROWS, FF), 0, 0).astype(BF)
        od[s] = dot(hid[...].reshape(ROWS, FF), gcol[s], 0, 0).astype(BF)
        pltpu.make_async_copy(ogu.at[s, 0], dg_o.at[at, :], gusem.at[s]).start()
        pltpu.make_async_copy(ogu.at[s, 1], du_o.at[at, :], gusem.at[s]).start()
        pltpu.make_async_copy(od.at[s], dd_o.at[:, at], dsem.at[s]).start()

        for h in range(2):
            d = 2 * i + h
            a = group_to(grp, d)
            landed(rr1.at[a], t1r.at[a])
            hot = jnp.where(spot == pos_ref[a, 0:1, :], 1.0, 0.0).astype(BF)
            for c in range(0, D, 512):
                s2[a, :, c : c + 512] = dot(hot, rr1[a, :, c : c + 512]).astype(BF)

            if h == 0:
                @pl.when(d > 0)
                def _():
                    send(s2.at[a], rr2.at[grp], t2s.at[d], t2r.at[grp], (a, own))

                @pl.when(d == 0)
                def _():
                    pltpu.make_async_copy(s2.at[a], rr2.at[a], t2r.at[a]).start()
            else:
                send(s2.at[a], rr2.at[grp], t2s.at[d], t2r.at[grp], (a, own))

    for a in range(NG):
        landed(rr2.at[a], t2r.at[a])
    for c in range(0, D, 512):
        rows = rr2[:, :, c : c + 512].reshape(NG * PG, 512)
        gin_o[:, c : c + 512] = dot(c_ref[...], rows, 0, 0).astype(BF)

    for s in range(2):
        landed(ogu.at[s], gusem.at[s])
        landed(od.at[s], dsem.at[s])
    for a in range(NG):
        landed(dx.at[a, pl.ds(0, (NJ - 1) * CAP)], t1s.at[a])
    for d in range(1, NG):
        landed(s2.at[group_to(grp, d)], t2s.at[d])


def body(tokens_in, out_grad, expert_ids, gate_weights, w_gate, w_up, w_down):
    hbm = pl.BlockSpec(memory_space=pl.ANY)
    vm = pl.BlockSpec(memory_space=pltpu.VMEM)
    sem = pltpu.SemaphoreType.DMA
    shape = jax.ShapeDtypeStruct
    wg, wu, wd = w_gate[0], w_up[0], w_down[0]
    xr, gr, hid, gg, ug, hots, pos = pl.pallas_call(
        dispatch_kernel,
        name="dispatch",
        out_shape=(
            shape((NG, NJ, CAP, D), BF), shape((NG, NJ, CAP, D), BF),
            shape((NG, T, FF), BF), shape((NG, T, FF), BF), shape((NG, T, FF), BF),
            shape((NG * PG, T), BF), shape((NG, 8, 128), I32),
        ),
        in_specs=[vm, vm, hbm, vm, hbm, hbm, hbm],
        out_specs=(hbm, hbm, hbm, hbm, hbm, vm, vm),
        scratch_shapes=[
            pltpu.VMEM((NJ, T, D), BF),
            pltpu.VMEM((NG, NJ, CAP, D), BF),
            pltpu.VMEM((NG, PG, D), BF),
            pltpu.VMEM((NG, PG, D), BF),
            pltpu.VMEM((NG, NJ * CAP, D), BF),
            pltpu.VMEM((2, 2 * NJ, CAP, D), BF),
            pltpu.VMEM((2, 2 * NJ, CAP, D), BF),
            pltpu.VMEM((D, FF), BF), pltpu.VMEM((D, FF), BF), pltpu.VMEM((FF, D), BF),
            pltpu.VMEM((2, 2, 3, T, FF), BF),
            pltpu.VMEM((NJ, NG, T), I32), pltpu.VMEM((NJ, NG, T), I32),
            pltpu.VMEM((NG, 8, 128), I32), pltpu.VMEM((NG, 8, 128), I32),
            pltpu.VMEM((E, T), I32), pltpu.VMEM((E, T), F32),
            sem((7,)), sem((NJ,)), sem((NJ,)), sem((NJ,)),
            sem((NG,)), sem((NG,)), sem((NG,)), sem((NG,)), sem((NG,)), sem((NG,)),
            sem((NG,)), sem((NG,)), sem((3,)), sem((2,)), sem((2,)), sem((2,)),
        ],
        compiler_params=pltpu.CompilerParams(
            collective_id=0, has_side_effects=True, vmem_limit_bytes=VMEM_LIMIT
        ),
    )(expert_ids.T, gate_weights.T, tokens_in, out_grad, wg, wu, wd)
    grad_in, d_gate, d_up, d_down = pl.pallas_call(
        combine_kernel,
        name="combine",
        out_shape=(
            shape((T, D), BF), shape((D, FF), BF), shape((D, FF), BF), shape((FF, D), BF),
        ),
        in_specs=[vm, vm] + [hbm] * 7,
        out_specs=(vm, hbm, hbm, hbm),
        scratch_shapes=[
            pltpu.VMEM((NG, T, FF), BF), pltpu.VMEM((NG, T, FF), BF), pltpu.VMEM((NG, T, FF), BF),
            pltpu.VMEM((D, FF), BF), pltpu.VMEM((D, FF), BF),
            pltpu.VMEM((NG, T, D), BF),
            pltpu.VMEM((NG, T, D), BF),
            pltpu.VMEM((NG, PG, D), BF),
            pltpu.VMEM((NG, PG, D), BF),
            pltpu.VMEM((2, ROWS, 256), BF), pltpu.VMEM((2, ROWS, 256), BF),
            pltpu.VMEM((2, 2, 256, FF), BF), pltpu.VMEM((2, FF, 256), BF),
            sem((5,)), sem((NG,)), sem((NG,)), sem((NG,)), sem((NG,)),
            sem((2,)), sem((2,)), sem((2,)), sem((2,)),
        ],
        compiler_params=pltpu.CompilerParams(
            collective_id=1, has_side_effects=True, vmem_limit_bytes=VMEM_LIMIT
        ),
    )(hots, pos, xr.reshape(ROWS, D), gr.reshape(ROWS, D), hid, gg, ug, wg, wu)
    return grad_in, d_gate[None], d_up[None], d_down[None]


def solution(mesh):
    both = ("group", "expert")
    return jax.shard_map(
        body,
        mesh=mesh,
        in_specs=(P(both, None),) * 4 + (P(both, None, None),) * 3,
        out_specs=(P(both, None),) + (P(both, None, None),) * 3,
        check_vma=False,
    )
```

time: 482 us -> 343 us (0.71); the launches traced: 473 us -> 343 us
  Pallas kernels: 0 us -> 332 us
  waiting for transfers between devices: 224 us -> 0 us
  local copies, waits for them, and re-layouts: 129 us -> 10.5 us
  matrix products: 56.5 us -> 0 us
  starting transfers between devices: 46.4 us -> 0 us
  other arithmetic: 15.3 us -> 0 us
    pallas_call x0 -> x2, Pallas kernels: none -> 332 us  [the longest x1 180 us: body(): pl.pallas_call(dispatch_kernel, name='dispatch', out_shape=(shape((NG, NJ...]
    all_to_all x4 -> x0, waiting for transfers between devices: 224 us -> none  [the longest x1 95.3 us: body(): lax.all_to_all(rows_grad.reshape(experts, capacity, model_width), ('group...]
    gather x12 -> x0, local copies, waits for them, and re-layouts: 126 us -> none  [the longest x1 19.1 us: body(): returned = jnp.where(kept[:, None], input_rows[back_pos], 0)]
    dot_general x11 -> x0, matrix products: 56.5 us -> none  [the longest x4 23.4 us: contract_rows(): lax.dot_general(first_op, second_op, (((0,), (0,)), ((), ())), preferred_...]
    all_to_all x4 -> x0, starting transfers between devices: 46.4 us -> none  [the longest x1 13 us: body(): lax.all_to_all(returned.reshape(experts, capacity, model_width), ('group'...]
    unnamed x36 -> x8, local copies, waits for them, and re-layouts: 1.94 us -> 10.5 us
    select_n x8 -> x0, other arithmetic: 7.51 us -> none  [the longest x2 7.44 us: body(): returned = jnp.where(kept[:, None], input_rows[back_pos], 0)]
  transfers between devices with their start and end apart: 4 -> 0, of which waited for: 3 -> 0; matrix products, arithmetic and copies ran while one was open for 28% -> 0% of each run, Pallas kernels for 0% -> 0%
where the time goes in v1:
time: 343 us
  Pallas kernels  332 us (97%)
  local copies, waits for them, and re-layouts  10.5 us (3%)
    pallas_call x1, Pallas kernels, body(): pl.pallas_call(dispatch_kernel, name='dispatch', out_shape=(shape((NG, NJ...  180 us
    pallas_call x1, Pallas kernels, body(): pl.pallas_call(combine_kernel, name='combine', out_shape=(shape((T, D), B...  151 us
    unnamed x8, local copies, waits for them, and re-layouts  10.5 us

profile of v1, /device:TPU:9, one launch (start us, length us, event | category | flops | bytes accessed | tf_op | source)
XLA Modules:
  0.0 342.7 jit_solution(2062068250064691628)
XLA Ops:
  0.6 180.1 %dispatch.1 = (bf16[16,8,16,2048]{3,2,1,0:T(8,128)(2,1)}, bf16[16,8,16,2048]{3,2,1,0:T(8,128)(2,1)}, bf16[16,128,768]{2,1,0:T(8,128)(2,1)}, bf16[16,128,768]{2,1...) custom-call(s32[8,128]{1,0:T(8,128)} %bitcast.20, ...), custom_call_target="tpu_custom_call" | custom-call | tf_op jit(solution)/shard_map/dispatch/pallas_call | solution.py:383
  180.7 151.5 %combine.1 = (bf16[128,2048]{1,0:T(8,128)(2,1)}, bf16[2048,768]{1,0:T(8,128)(2,1)}, bf16[2048,768]{1,0:T(8,128)(2,1)}, bf16[768,2048]{1,0:T(8,128)(2,1)}) custom-call(bf16[1024,128]{1,0:T(8,128)(2,1)} %get-tuple-element.15.c_ref, s32[16,8,128]{2,1,0:T(8,128)} %get-tuple-element.16.pos_ref, bf16[2048,2048]{1,0:T(8,128)(2,1)} %bitcast.14, ...), custom_call_target="tpu_custom_call" | custom-call | tf_op jit(solution)/shard_map/combine/pallas_call | solution.py:414
  332.2 1.9 copy.15
  334.1 0.0 copy-start.1
  334.1 3.9 %copy.16 = bf16[1,2048,768]{2,1,0:T(8,128)(2,1)} copy(bf16[1,2048,768]{2,1,0:T(8,128)(2,1)} %bitcast.18) | data formatting | bytes 6291456
  338.0 0.0 copy-done.1
  338.0 0.0 copy-start
  338.0 1.7 copy.17
  339.7 1.4 copy-done
  341.1 1.7 copy.18
Async XLA Ops:
  334.1 3.9 %copy-start.1 = (bf16[2048,768]{1,0:T(8,128)(2,1)S(1)}, bf16[2048,768]{1,0:T(8,128)(2,1)}, u32[]{:S(2)}) copy-start(bf16[2048,768]{1,0:T(8,128)(2,1)} %get-tuple-element.24) | copy-start | bytes 9437188
  338.0 3.0 copy-start

commit v2 on v1

--- a/solution.py
+++ b/solution.py
@@ -20,7 +20,17 @@
     return lax.dot_general(a, b, (((ca,), (cb,)), ((), ())), preferred_element_type=F32)
 
 
+NEAR = ((0, 1), (1, 0), (0, 3), (3, 0))
+DIAG = ((1, 1), (3, 3), (1, 3), (3, 1))
+LONG = ((1, 2), (2, 1), (3, 2), (2, 3))
+FAR = ((2, 2), (0, 2), (2, 0))
+SETS = (NEAR, DIAG, LONG, FAR + ((0, 0),))
+OUTWARD = FAR[:1] + LONG + FAR[1:] + DIAG + NEAR
+
+
 def shift_of(d):
+    if isinstance(d, tuple):
+        return d
     if isinstance(d, int):
         return d % 4, (d // 4 + d % 4) % 4
     dy = lax.rem(d, 4)
@@ -124,10 +134,10 @@
     send(x_hbm, ax.at[own], axs.at[0], axr.at[own], (grp, partner))
 
     spot = iota((PG, T), 0)
-    for b in range(4):
+    for steps in SETS:
         picks, scales = [], []
-        for q in range(4):
-            a = group_to(grp, 4 * b + q)
+        for d in steps:
+            a = group_to(grp, d)
             at = pl.ds(pl.multiple_of(a * NJ, NJ), NJ)
             prow, wrow = post[at, :], wt[at, :]
             hot = jnp.zeros((PG, T), F32)
@@ -143,15 +153,17 @@
         scale = jnp.concatenate(scales, axis=0)
         for c in range(0, D, 512):
             part = (scale * dot(hots, g_ref[:, c : c + 512])).astype(BF)
-            for q in range(4):
-                s1[group_to(grp, 4 * b + q), :, c : c + 512] = part[q * PG : (q + 1) * PG, :]
-        for q in range(4):
-            d = 4 * b + q
-            if d == 0:
-                continue
+            for q, d in enumerate(steps):
+                s1[group_to(grp, d), :, c : c + 512] = part[q * PG : (q + 1) * PG, :]
+        ends = [d for d in steps if d != (0, 0)]
+        for d in ends:
             a = group_to(grp, d)
-            send(pos_s.at[a], pos_r.at[grp], ps.at[d], pr.at[grp], (a, own))
-            send(s1.at[a], r1.at[grp], q1s.at[d], q1r.at[grp], (a, own))
+            send(pos_s.at[a], pos_r.at[grp], ps.at[a], pr.at[grp], (a, own))
+        for r in range(0, PG, 16):
+            for d in ends:
+                a = group_to(grp, d)
+                send(s1.at[a, pl.ds(r, 16)], r1.at[grp, pl.ds(r, 16)],
+                     q1s.at[a], q1r.at[grp], (a, own))
     for w in loads:
         w.start()
 
@@ -162,28 +174,31 @@
         for k in range(1, NJ):
             to = lax.rem(own + k, NJ)
             at = pl.ds(pl.multiple_of(to * CAP, CAP), CAP)
-            send(s2.at[a, at], gr.at[a, own], q2s.at[a], q2r.at[a], (grp, to))
+            send(s2.at[a, at], gr.at[own, a], q2s.at[a], q2r.at[own], (grp, to))
         at = pl.ds(pl.multiple_of(own * CAP, CAP), CAP)
-        pltpu.make_async_copy(s2.at[a, at], gr.at[a, own], q2r.at[a]).start()
+        pltpu.make_async_copy(s2.at[a, at], gr.at[own, a], q2r.at[own]).start()
 
     spread(grp, s1)
 
-    for i in range(1, 4):
-        slot_i = lax.rem(own - 2 * i + NJ, NJ)
-        landed(ax.at[slot_i], axr.at[slot_i])
-        send(ax.at[slot_i], ax.at[slot_i], axs.at[3 + i], axr.at[slot_i], (grp, partner))
-    for i in range(4):
-        slot_i = lax.rem(partner + 2 * i, NJ)
-        landed(ax.at[slot_i], axr.at[slot_i])
-    landed(ax.at[own], axr.at[own])
     for k in range(1, NJ):
         frm = lax.rem(own + k, NJ)
         landed(rank_r.at[frm], mr.at[frm])
 
     cap_row = iota((CAP, T), 0)
 
+    def source(n):
+        side = lax.rem(n, 2)
+        return lax.rem(own + (partner - own) * side - (n - side) + NJ, NJ)
+
     @pl.loop(0, NJ)
-    def _(j):
+    def _(n):
+        j = source(n)
+        landed(ax.at[j], axr.at[j])
+
+        @pl.when((n >= 2) & (lax.rem(n, 2) == 0))
+        def _():
+            send(ax.at[j], ax.at[j], axs.at[3 + lax.div(n, 2)], axr.at[j], (grp, partner))
+
         hots = jnp.concatenate(
             [
                 jnp.where(cap_row == rank_r[j, a : a + 1, :], 1.0, 0.0).astype(BF)
@@ -193,45 +208,39 @@
         )
         for c in range(0, D, 512):
             part = dot(hots, ax[j, :, c : c + 512]).astype(BF)
-            pbuf[:, j, :, c : c + 512] = part.reshape(NG, CAP, 512)
-
-    for d in range(1, NG):
-        a = group_to(grp, d)
-        send(pbuf.at[a], xr.at[grp], p2s.at[d], p2r.at[grp], (a, own))
-    pltpu.make_async_copy(pbuf.at[grp], xr.at[grp], p2r.at[grp]).start()
-
-    @pl.loop(1, NG)
-    def _(d):
-        a = group_from(grp, d)
-        landed(pos_r.at[a], pr.at[a])
-        landed(r1.at[a], q1r.at[a])
-        spread(a, r1)
+            pbuf[j, :, :, c : c + 512] = part.reshape(NG, CAP, 512)
+        for d in OUTWARD:
+            a = group_to(grp, d)
+            send(pbuf.at[j, a], xr.at[j, grp], p2s.at[j], p2r.at[j], (a, own))
+        pltpu.make_async_copy(pbuf.at[j, grp], xr.at[j, grp], p2r.at[j]).start()
+
+    for steps in SETS:
+        for d in steps:
+            if d != (0, 0):
+                a = group_from(grp, d)
+                landed(pos_r.at[a], pr.at[a])
+                landed(r1.at[a], q1r.at[a])
+                spread(a, r1)
 
     for w in loads:
         w.wait()
 
-    def fetch(i, s):
-        for h in range(2):
-            a = group_from(grp, 2 * i + h)
-            landed(xr.at[a], p2r.at[a])
-            landed(gr.at[a], q2r.at[a])
-            pltpu.make_async_copy(xr.at[a], stx.at[s, pl.ds(h * NJ, NJ)], xsem.at[s]).start()
-            pltpu.make_async_copy(gr.at[a], stg.at[s, pl.ds(h * NJ, NJ)], gsem.at[s]).start()
-
-    fetch(0, 0)
-
-    @pl.loop(0, NG // 2)
-    def _(i):
-        s = lax.rem(i, 2)
-
-        @pl.when(i >= 2)
+    def fetch(n, s):
+        j = source(n)
+        landed(xr.at[j], p2r.at[j])
+        landed(gr.at[j], q2r.at[j])
+        pltpu.make_async_copy(xr.at[j], stx.at[s], xsem.at[s]).start()
+        pltpu.make_async_copy(gr.at[j], stg.at[s], gsem.at[s]).start()
+
+    @pl.loop(0, NJ)
+    def _(n):
+        s = lax.rem(n, 2)
+
+        @pl.when(n >= 2)
         def _():
             landed(ost.at[s], osem.at[s])
 
-        @pl.when(i + 1 < NG // 2)
-        def _():
-            fetch(i + 1, 1 - s)
-
+        fetch(n, s)
         landed(stx.at[s], xsem.at[s])
         landed(stg.at[s], gsem.at[s])
         xb = stx[s].reshape(2 * T, D)
@@ -241,14 +250,11 @@
         hgrad = dot(gb, wd[...], 1, 1)
         sigma = jax.nn.sigmoid(gate_pre)
         act = gate_pre * sigma
-        hid = (act * up_pre).astype(BF)
-        gg = (hgrad * up_pre * sigma * (1.0 + gate_pre * (1.0 - sigma))).astype(BF)
-        ug = (hgrad * act).astype(BF)
-        for h in range(2):
-            a = group_from(grp, 2 * i + h)
-            for n, (val, out) in enumerate(((hid, hid_o), (gg, gg_o), (ug, ug_o))):
-                ost[s, h, n] = val[h * T : (h + 1) * T, :]
-                pltpu.make_async_copy(ost.at[s, h, n], out.at[a], osem.at[s]).start()
+        ost[s, 0] = (act * up_pre).astype(BF)
+        ost[s, 1] = (hgrad * up_pre * sigma * (1.0 + gate_pre * (1.0 - sigma))).astype(BF)
+        ost[s, 2] = (hgrad * act).astype(BF)
+        for v, out in enumerate((hid_o, gg_o, ug_o)):
+            pltpu.make_async_copy(ost.at[s, v], out.at[source(n)], osem.at[s]).start()
 
     pos_o[...] = pos_r[...]
     for s in range(2):
@@ -260,9 +266,10 @@
         landed(x_hbm, axs.at[i])
     for d in range(1, NG):
         a = group_to(grp, d)
-        landed(pos_s.at[a], ps.at[d])
-        landed(s1.at[a], q1s.at[d])
-        landed(pbuf.at[a], p2s.at[d])
+        landed(pos_s.at[a], ps.at[a])
+        landed(s1.at[a], q1s.at[a])
+    for j in range(NJ):
+        landed(pbuf.at[j, pl.ds(0, NG - 1)], p2s.at[j])
     for a in range(NG):
         landed(s2.at[a, pl.ds(0, (NJ - 1) * CAP)], q2s.at[a])
 
@@ -290,8 +297,9 @@
     @pl.loop(0, NG // 2)
     def _(i):
         tops = [group_to(grp, 2 * i + h) for h in range(2)]
-        ggb = jnp.concatenate([gg[a] for a in tops], axis=0)
-        ugb = jnp.concatenate([ug[a] for a in tops], axis=0)
+        ats = [pl.ds(pl.multiple_of(a * CAP, CAP), CAP) for a in tops]
+        ggb = jnp.concatenate([gg[j, at, :] for at in ats for j in range(NJ)], axis=0)
+        ugb = jnp.concatenate([ug[j, at, :] for at in ats for j in range(NJ)], axis=0)
         for c in range(0, D, 512):
             part = dot(ggb, wg[c : c + 512, :], 1, 1) + dot(ugb, wu[c : c + 512, :], 1, 1)
             part = part.astype(BF)
@@ -384,22 +392,22 @@
         dispatch_kernel,
         name="dispatch",
         out_shape=(
-            shape((NG, NJ, CAP, D), BF), shape((NG, NJ, CAP, D), BF),
-            shape((NG, T, FF), BF), shape((NG, T, FF), BF), shape((NG, T, FF), BF),
+            shape((NJ, NG, CAP, D), BF), shape((NJ, NG, CAP, D), BF),
+            shape((NJ, 2 * T, FF), BF), shape((NJ, 2 * T, FF), BF), shape((NJ, 2 * T, FF), BF),
             shape((NG * PG, T), BF), shape((NG, 8, 128), I32),
         ),
         in_specs=[vm, vm, hbm, vm, hbm, hbm, hbm],
         out_specs=(hbm, hbm, hbm, hbm, hbm, vm, vm),
         scratch_shapes=[
             pltpu.VMEM((NJ, T, D), BF),
-            pltpu.VMEM((NG, NJ, CAP, D), BF),
+            pltpu.VMEM((NJ, NG, CAP, D), BF),
             pltpu.VMEM((NG, PG, D), BF),
             pltpu.VMEM((NG, PG, D), BF),
             pltpu.VMEM((NG, NJ * CAP, D), BF),
-            pltpu.VMEM((2, 2 * NJ, CAP, D), BF),
-            pltpu.VMEM((2, 2 * NJ, CAP, D), BF),
+            pltpu.VMEM((2, NG, CAP, D), BF),
+            pltpu.VMEM((2, NG, CAP, D), BF),
             pltpu.VMEM((D, FF), BF), pltpu.VMEM((D, FF), BF), pltpu.VMEM((FF, D), BF),
-            pltpu.VMEM((2, 2, 3, T, FF), BF),
+            pltpu.VMEM((2, 3, 2 * T, FF), BF),
             pltpu.VMEM((NJ, NG, T), I32), pltpu.VMEM((NJ, NG, T), I32),
             pltpu.VMEM((NG, 8, 128), I32), pltpu.VMEM((NG, 8, 128), I32),
             pltpu.VMEM((E, T), I32), pltpu.VMEM((E, T), F32),
@@ -420,7 +428,8 @@
         in_specs=[vm, vm] + [hbm] * 7,
         out_specs=(vm, hbm, hbm, hbm),
         scratch_shapes=[
-            pltpu.VMEM((NG, T, FF), BF), pltpu.VMEM((NG, T, FF), BF), pltpu.VMEM((NG, T, FF), BF),
+            pltpu.VMEM((NJ, 2 * T, FF), BF), pltpu.VMEM((NJ, 2 * T, FF), BF),
+            pltpu.VMEM((NJ, 2 * T, FF), BF),
             pltpu.VMEM((D, FF), BF), pltpu.VMEM((D, FF), BF),
             pltpu.VMEM((NG, T, D), BF),
             pltpu.VMEM((NG, T, D), BF),

time: 343 us -> 281 us (0.82)
  Pallas kernels: 332 us -> 267 us
    pallas_call x1, Pallas kernels: 151 us -> 114 us  [body(): pl.pallas_call(combine_kernel, name='combine', out_shape=(shape((T, D), B...]
    pallas_call x1, Pallas kernels: 180 us -> 154 us  [body(): pl.pallas_call(dispatch_kernel, name='dispatch', out_shape=(shape((NJ, NG...]
where the time goes in v2:
time: 281 us; the launch traced here: 279 us
  Pallas kernels  267 us (95%)
  local copies, waits for them, and re-layouts  10.5 us (4%)
    pallas_call x1, Pallas kernels, body(): pl.pallas_call(dispatch_kernel, name='dispatch', out_shape=(shape((NJ, NG...  154 us
    pallas_call x1, Pallas kernels, body(): pl.pallas_call(combine_kernel, name='combine', out_shape=(shape((T, D), B...  114 us
    unnamed x8, local copies, waits for them, and re-layouts  10.5 us

profile of v2, /device:TPU:9, one launch (start us, length us, event | category | flops | bytes accessed | tf_op | source)
XLA Modules:
  0.0 278.5 jit_solution(5087123452067219015)
XLA Ops:
  0.6 153.8 %dispatch.1 = (bf16[8,16,16,2048]{3,2,1,0:T(8,128)(2,1)}, bf16[8,16,16,2048]{3,2,1,0:T(8,128)(2,1)}, bf16[8,256,768]{2,1,0:T(8,128)(2,1)}, bf16[8,256,768]{2,1,0...) custom-call(s32[8,128]{1,0:T(8,128)} %bitcast.20, ...), custom_call_target="tpu_custom_call" | custom-call | tf_op jit(solution)/shard_map/dispatch/pallas_call | solution.py:391
  154.4 113.6 %combine.1 = (bf16[128,2048]{1,0:T(8,128)(2,1)}, bf16[2048,768]{1,0:T(8,128)(2,1)}, bf16[2048,768]{1,0:T(8,128)(2,1)}, bf16[768,2048]{1,0:T(8,128)(2,1)}) custom-call(bf16[1024,128]{1,0:T(8,128)(2,1)} %get-tuple-element.15.c_ref, s32[16,8,128]{2,1,0:T(8,128)} %get-tuple-element.16.pos_ref, bf16[2048,2048]{1,0:T(8,128)(2,1)} %bitcast.14, ...), custom_call_target="tpu_custom_call" | custom-call | tf_op jit(solution)/shard_map/combine/pallas_call | solution.py:422
  268.0 1.9 copy.15
  269.9 0.0 copy-start.1
  269.9 3.9 %copy.16 = bf16[1,2048,768]{2,1,0:T(8,128)(2,1)} copy(bf16[1,2048,768]{2,1,0:T(8,128)(2,1)} %bitcast.18) | data formatting | bytes 6291456
  273.8 0.0 copy-done.1
  273.8 0.0 copy-start
  273.8 1.7 copy.17
  275.5 1.4 copy-done
  276.8 1.7 copy.18
Async XLA Ops:
  269.9 3.9 %copy-start.1 = (bf16[2048,768]{1,0:T(8,128)(2,1)S(1)}, bf16[2048,768]{1,0:T(8,128)(2,1)}, u32[]{:S(2)}) copy-start(bf16[2048,768]{1,0:T(8,128)(2,1)} %get-tuple-element.24) | copy-start | bytes 9437188
  273.8 3.0 %copy-start = (bf16[768,2048]{1,0:T(8,128)(2,1)S(1)}, bf16[768,2048]{1,0:T(8,128)(2,1)}, u32[]{:S(2)}) copy-start(bf16[768,2048]{1,0:T(8,128)(2,1)} %get-tuple-element.25) | copy-start | bytes 9437188

commit v3 on v2

--- a/solution.py
+++ b/solution.py
@@ -10,6 +10,7 @@
 CAP = 16
 PG = 64
 E = NG * NJ
+DP = 1024
 ROWS = NG * NJ * CAP
 BF, F32, I32 = jnp.bfloat16, jnp.float32, jnp.int32
 MESH = pl.DeviceIdType.MESH
@@ -73,9 +74,17 @@
     return lax.broadcasted_iota(I32, shape, dim)
 
 
+def slots_of(rank_ref, j):
+    spot = iota((CAP, T), 0)
+    return jnp.concatenate(
+        [jnp.where(spot == rank_ref[j, a : a + 1, :], 1.0, 0.0).astype(BF) for a in range(NG)],
+        axis=0,
+    )
+
+
 def dispatch_kernel(
     ids_ref, gw_ref, x_hbm, g_ref, wg_hbm, wu_hbm, wd_hbm,
-    xr, gr, hid_o, gg_o, ug_o, c_o, pos_o,
+    xr, gr, hid_o, gg_o, ug_o, c_o, pos_o, rank_o,
     ax, pbuf, s1, r1, s2, stx, stg, wg, wu, wd, ost,
     rank_s, rank_r, pos_s, pos_r, post, wt,
     axs, axr, ms, mr, ps, pr, q1s, q1r, q2s, q2r, p2s, p2r, wsem, xsem, gsem, osem,
@@ -184,8 +193,6 @@
         frm = lax.rem(own + k, NJ)
         landed(rank_r.at[frm], mr.at[frm])
 
-    cap_row = iota((CAP, T), 0)
-
     def source(n):
         side = lax.rem(n, 2)
         return lax.rem(own + (partner - own) * side - (n - side) + NJ, NJ)
@@ -199,13 +206,7 @@
         def _():
             send(ax.at[j], ax.at[j], axs.at[3 + lax.div(n, 2)], axr.at[j], (grp, partner))
 
-        hots = jnp.concatenate(
-            [
-                jnp.where(cap_row == rank_r[j, a : a + 1, :], 1.0, 0.0).astype(BF)
-                for a in range(NG)
-            ],
-            axis=0,
-        )
+        hots = slots_of(rank_r, j)
         for c in range(0, D, 512):
             part = dot(hots, ax[j, :, c : c + 512]).astype(BF)
             pbuf[j, :, :, c : c + 512] = part.reshape(NG, CAP, 512)
@@ -257,6 +258,7 @@
             pltpu.make_async_copy(ost.at[s, v], out.at[source(n)], osem.at[s]).start()
 
     pos_o[...] = pos_r[...]
+    rank_o[...] = rank_r[...]
     for s in range(2):
         landed(ost.at[s], osem.at[s])
     for k in range(1, NJ):
@@ -275,10 +277,10 @@
 
 
 def combine_kernel(
-    c_ref, pos_ref, xr, gr, hid_hbm, gg_hbm, ug_hbm, wg_hbm, wu_hbm,
+    c_ref, pos_ref, rank_ref, xr, gr, hid_hbm, gg_hbm, ug_hbm, wg_hbm, wu_hbm,
     gin_o, dg_o, du_o, dd_o,
-    hid, gg, ug, wg, wu, dx, rr1, s2, rr2, xcol, gcol, ogu, od,
-    lsem, t1s, t1r, t2s, t2r, xsem, gsem, gusem, dsem,
+    hid, gg, ug, wg, wu, dxp, dxq, rrp, rrq, part, rrz, s2, rr2, xcol, gcol, ogu, od,
+    lsem, p1s, p1r, p2s, p2r, t1s, t1r, t2s, t2r, xsem, gsem, gusem, dsem,
 ):
     grp, own = lax.axis_index("group"), lax.axis_index("expert")
     barrier = enter(grp, own)
@@ -294,25 +296,43 @@
         w.wait()
     pl.semaphore_wait(barrier, NG + NJ - 2)
 
-    @pl.loop(0, NG // 2)
-    def _(i):
-        tops = [group_to(grp, 2 * i + h) for h in range(2)]
-        ats = [pl.ds(pl.multiple_of(a * CAP, CAP), CAP) for a in tops]
-        ggb = jnp.concatenate([gg[j, at, :] for at in ats for j in range(NJ)], axis=0)
-        ugb = jnp.concatenate([ug[j, at, :] for at in ats for j in range(NJ)], axis=0)
-        for c in range(0, D, 512):
-            part = dot(ggb, wg[c : c + 512, :], 1, 1) + dot(ugb, wu[c : c + 512, :], 1, 1)
-            part = part.astype(BF)
+    def slot_rows(a):
+        return pl.ds(pl.multiple_of(a * CAP, CAP), CAP)
+
+    def input_rows(ggb, ugb, c):
+        return (
+            dot(ggb, wg[c : c + 512, :], 1, 1) + dot(ugb, wu[c : c + 512, :], 1, 1)
+        ).astype(BF)
+
+    @pl.loop(0, NJ)
+    def _(n):
+        j = lax.rem(own + 4 + n, NJ)
+        for c in range(0, DP, 512):
+            dxp[j, :, c : c + 512] = input_rows(gg[j], ug[j], c)
+        for d in OUTWARD:
+            a = group_to(grp, d)
+            send(dxp.at[j, slot_rows(a)], rrp.at[j, slot_rows(grp)],
+                 p1s.at[j], p1r.at[j], (a, own))
+        pltpu.make_async_copy(
+            dxp.at[j, slot_rows(grp)], rrp.at[j, slot_rows(grp)], p1r.at[j]
+        ).start()
+
+        tops = [group_to(grp, 2 * n + h) for h in range(2)]
+        ats = [slot_rows(a) for a in tops]
+        ggb = jnp.concatenate([gg[q, at, :] for at in ats for q in range(NJ)], axis=0)
+        ugb = jnp.concatenate([ug[q, at, :] for at in ats for q in range(NJ)], axis=0)
+        for c in range(DP, D, 512):
+            rows = input_rows(ggb, ugb, c)
             for h in range(2):
-                dx[tops[h], :, c : c + 512] = part[h * T : (h + 1) * T, :]
+                dxq[tops[h], :, c - DP : c - DP + 512] = rows[h * T : (h + 1) * T, :]
         for a in tops:
             for k in range(1, NJ):
                 to = lax.rem(own + k, NJ)
-                at = pl.ds(pl.multiple_of(to * CAP, CAP), CAP)
-                back = pl.ds(pl.multiple_of(own * CAP, CAP), CAP)
-                send(dx.at[a, at], rr1.at[a, back], t1s.at[a], t1r.at[a], (grp, to))
-            at = pl.ds(pl.multiple_of(own * CAP, CAP), CAP)
-            pltpu.make_async_copy(dx.at[a, at], rr1.at[a, at], t1r.at[a]).start()
+                send(dxq.at[a, slot_rows(to)], rrq.at[a, slot_rows(own)],
+                     t1s.at[a], t1r.at[a], (grp, to))
+            pltpu.make_async_copy(
+                dxq.at[a, slot_rows(own)], rrq.at[a, slot_rows(own)], t1r.at[a]
+            ).start()
 
     loads[4].wait()
     spot = iota((PG, T), 0)
@@ -324,7 +344,7 @@
 
     fetch(0, 0)
 
-    @pl.loop(0, NG // 2)
+    @pl.loop(0, NJ)
     def _(i):
         s = lax.rem(i, 2)
 
@@ -333,7 +353,7 @@
             landed(ogu.at[s], gusem.at[s])
             landed(od.at[s], dsem.at[s])
 
-        @pl.when(i + 1 < NG // 2)
+        @pl.when(i + 1 < NJ)
         def _():
             fetch(i + 1, 1 - s)
 
@@ -348,38 +368,65 @@
         pltpu.make_async_copy(ogu.at[s, 1], du_o.at[at, :], gusem.at[s]).start()
         pltpu.make_async_copy(od.at[s], dd_o.at[:, at], dsem.at[s]).start()
 
+        j = lax.rem(own + 4 + i, NJ)
+        landed(rrp.at[j], p1r.at[j])
+        hots = slots_of(rank_ref, j)
+        for c in range(0, DP, 512):
+            part[j, :, c : c + 512] = dot(hots, rrp[j, :, c : c + 512], 0, 0).astype(BF)
+
+        @pl.when(i != 4)
+        def _():
+            send(part.at[j], rrz.at[own], p2s.at[j], p2r.at[own], (grp, j))
+
+        @pl.when(i == 4)
+        def _():
+            pltpu.make_async_copy(part.at[j], rrz.at[j], p2r.at[j]).start()
+
         for h in range(2):
             d = 2 * i + h
             a = group_to(grp, d)
-            landed(rr1.at[a], t1r.at[a])
+            landed(rrq.at[a], t1r.at[a])
             hot = jnp.where(spot == pos_ref[a, 0:1, :], 1.0, 0.0).astype(BF)
-            for c in range(0, D, 512):
-                s2[a, :, c : c + 512] = dot(hot, rr1[a, :, c : c + 512]).astype(BF)
+            for c in range(0, D - DP, 512):
+                s2[a, :, c : c + 512] = dot(hot, rrq[a, :, c : c + 512]).astype(BF)
 
             if h == 0:
                 @pl.when(d > 0)
                 def _():
-                    send(s2.at[a], rr2.at[grp], t2s.at[d], t2r.at[grp], (a, own))
+                    send(s2.at[a], rr2.at[grp], t2s.at[a], t2r.at[grp], (a, own))
 
                 @pl.when(d == 0)
                 def _():
                     pltpu.make_async_copy(s2.at[a], rr2.at[a], t2r.at[a]).start()
             else:
-                send(s2.at[a], rr2.at[grp], t2s.at[d], t2r.at[grp], (a, own))
-
+                send(s2.at[a], rr2.at[grp], t2s.at[a], t2r.at[grp], (a, own))
+
+    for j in range(NJ):
+        landed(rrz.at[j], p2r.at[j])
+    for c in range(0, DP, 512):
+        total = rrz[0, :, c : c + 512].astype(F32)
+        for j in range(1, NJ):
+            total = total + rrz[j, :, c : c + 512].astype(F32)
+        gin_o[:, c : c + 512] = total.astype(BF)
     for a in range(NG):
         landed(rr2.at[a], t2r.at[a])
-    for c in range(0, D, 512):
+    for c in range(0, D - DP, 512):
         rows = rr2[:, :, c : c + 512].reshape(NG * PG, 512)
-        gin_o[:, c : c + 512] = dot(c_ref[...], rows, 0, 0).astype(BF)
+        gin_o[:, DP + c : DP + c + 512] = dot(c_ref[...], rows, 0, 0).astype(BF)
 
     for s in range(2):
         landed(ogu.at[s], gusem.at[s])
         landed(od.at[s], dsem.at[s])
     for a in range(NG):
-        landed(dx.at[a, pl.ds(0, (NJ - 1) * CAP)], t1s.at[a])
+        landed(dxq.at[a, pl.ds(0, (NJ - 1) * CAP)], t1s.at[a])
+    for j in range(NJ):
+        landed(dxp.at[j, pl.ds(0, (NG - 1) * CAP)], p1s.at[j])
+    for k in range(1, NJ):
+        j = lax.rem(own + k, NJ)
+        landed(part.at[j], p2s.at[j])
     for d in range(1, NG):
-        landed(s2.at[group_to(grp, d)], t2s.at[d])
+        a = group_to(grp, d)
+        landed(s2.at[a], t2s.at[a])
 
 
 def body(tokens_in, out_grad, expert_ids, gate_weights, w_gate, w_up, w_down):
@@ -388,16 +435,16 @@
     sem = pltpu.SemaphoreType.DMA
     shape = jax.ShapeDtypeStruct
     wg, wu, wd = w_gate[0], w_up[0], w_down[0]
-    xr, gr, hid, gg, ug, hots, pos = pl.pallas_call(
+    xr, gr, hid, gg, ug, hots, pos, rank = pl.pallas_call(
         dispatch_kernel,
         name="dispatch",
         out_shape=(
             shape((NJ, NG, CAP, D), BF), shape((NJ, NG, CAP, D), BF),
             shape((NJ, 2 * T, FF), BF), shape((NJ, 2 * T, FF), BF), shape((NJ, 2 * T, FF), BF),
-            shape((NG * PG, T), BF), shape((NG, 8, 128), I32),
+            shape((NG * PG, T), BF), shape((NG, 8, 128), I32), shape((NJ, NG, T), I32),
         ),
         in_specs=[vm, vm, hbm, vm, hbm, hbm, hbm],
-        out_specs=(hbm, hbm, hbm, hbm, hbm, vm, vm),
+        out_specs=(hbm, hbm, hbm, hbm, hbm, vm, vm, vm),
         scratch_shapes=[
             pltpu.VMEM((NJ, T, D), BF),
             pltpu.VMEM((NJ, NG, CAP, D), BF),
@@ -425,25 +472,30 @@
         out_shape=(
             shape((T, D), BF), shape((D, FF), BF), shape((D, FF), BF), shape((FF, D), BF),
         ),
-        in_specs=[vm, vm] + [hbm] * 7,
+        in_specs=[vm, vm, vm] + [hbm] * 7,
         out_specs=(vm, hbm, hbm, hbm),
         scratch_shapes=[
             pltpu.VMEM((NJ, 2 * T, FF), BF), pltpu.VMEM((NJ, 2 * T, FF), BF),
             pltpu.VMEM((NJ, 2 * T, FF), BF),
             pltpu.VMEM((D, FF), BF), pltpu.VMEM((D, FF), BF),
-            pltpu.VMEM((NG, T, D), BF),
-            pltpu.VMEM((NG, T, D), BF),
-            pltpu.VMEM((NG, PG, D), BF),
-            pltpu.VMEM((NG, PG, D), BF),
+            pltpu.VMEM((NJ, 2 * T, DP), BF),
+            pltpu.VMEM((NG, T, D - DP), BF),
+            pltpu.VMEM((NJ, 2 * T, DP), BF),
+            pltpu.VMEM((NG, T, D - DP), BF),
+            pltpu.VMEM((NJ, T, DP), BF),
+            pltpu.VMEM((NJ, T, DP), BF),
+            pltpu.VMEM((NG, PG, D - DP), BF),
+            pltpu.VMEM((NG, PG, D - DP), BF),
             pltpu.VMEM((2, ROWS, 256), BF), pltpu.VMEM((2, ROWS, 256), BF),
             pltpu.VMEM((2, 2, 256, FF), BF), pltpu.VMEM((2, FF, 256), BF),
-            sem((5,)), sem((NG,)), sem((NG,)), sem((NG,)), sem((NG,)),
+            sem((5,)), sem((NJ,)), sem((NJ,)), sem((NJ,)), sem((NJ,)),
+            sem((NG,)), sem((NG,)), sem((NG,)), sem((NG,)),
             sem((2,)), sem((2,)), sem((2,)), sem((2,)),
         ],
         compiler_params=pltpu.CompilerParams(
             collective_id=1, has_side_effects=True, vmem_limit_bytes=VMEM_LIMIT
         ),
-    )(hots, pos, xr.reshape(ROWS, D), gr.reshape(ROWS, D), hid, gg, ug, wg, wu)
+    )(hots, pos, rank, xr.reshape(ROWS, D), gr.reshape(ROWS, D), hid, gg, ug, wg, wu)
     return grad_in, d_gate[None], d_up[None], d_down[None]
 
 

time: 281 us -> 250 us (0.89)
  Pallas kernels: 267 us -> 236 us
    pallas_call x1, Pallas kernels: 114 us -> 82 us  [body(): pl.pallas_call(combine_kernel, name='combine', out_shape=(shape((T, D), B...]
where the time goes in v3:
time: 250 us; the launch traced here: 247 us
  Pallas kernels  236 us (94%)
  local copies, waits for them, and re-layouts  10.5 us (4%)
    pallas_call x1, Pallas kernels, body(): pl.pallas_call(dispatch_kernel, name='dispatch', out_shape=(shape((NJ, NG...  154 us
    pallas_call x1, Pallas kernels, body(): pl.pallas_call(combine_kernel, name='combine', out_shape=(shape((T, D), B...  82 us
    unnamed x8, local copies, waits for them, and re-layouts  10.5 us

profile of v3, /device:TPU:9, one launch (start us, length us, event | category | flops | bytes accessed | tf_op | source)
XLA Modules:
  0.0 247.0 jit_solution(2537837973363317781)
XLA Ops:
  0.6 153.8 %dispatch.1 = (bf16[8,16,16,2048]{3,2,1,0:T(8,128)(2,1)}, bf16[8,16,16,2048]{3,2,1,0:T(8,128)(2,1)}, bf16[8,256,768]{2,1,0:T(8,128)(2,1)}, bf16[8,256,768]{2,1,0...) custom-call(s32[8,128]{1,0:T(8,128)} %bitcast.20, ...), custom_call_target="tpu_custom_call" | custom-call | tf_op jit(solution)/shard_map/dispatch/pallas_call | solution.py:438
  154.5 82.0 %combine.1 = (bf16[128,2048]{1,0:T(8,128)(2,1)}, bf16[2048,768]{1,0:T(8,128)(2,1)}, bf16[2048,768]{1,0:T(8,128)(2,1)}, bf16[768,2048]{1,0:T(8,128)(2,1)}) custom-call(bf16[1024,128]{1,0:T(8,128)(2,1)} %get-tuple-element.16.c_ref, s32[16,8,128]{2,1,0:T(8,128)} %get-tuple-element.17.pos_ref, s32[8,16,128]{2,1,0:T(8,128)} %get-tuple-element.18.rank_ref, ...), custom_call_target="tpu_custom_call" | custom-call | tf_op jit(solution)/shard_map/combine/pallas_call | solution.py:469
  236.5 1.9 copy.15
  238.4 0.0 copy-start.1
  238.4 3.9 %copy.16 = bf16[1,2048,768]{2,1,0:T(8,128)(2,1)} copy(bf16[1,2048,768]{2,1,0:T(8,128)(2,1)} %bitcast.18) | data formatting | bytes 6291456
  242.3 0.0 copy-done.1
  242.3 0.0 copy-start
  242.3 1.7 copy.17
  244.0 1.4 copy-done
  245.3 1.7 copy.18
Async XLA Ops:
  238.4 3.9 %copy-start.1 = (bf16[2048,768]{1,0:T(8,128)(2,1)S(1)}, bf16[2048,768]{1,0:T(8,128)(2,1)}, u32[]{:S(2)}) copy-start(bf16[2048,768]{1,0:T(8,128)(2,1)} %get-tuple-element.26) | copy-start | bytes 9437188
  242.3 3.0 %copy-start = (bf16[768,2048]{1,0:T(8,128)(2,1)S(1)}, bf16[768,2048]{1,0:T(8,128)(2,1)}, u32[]{:S(2)}) copy-start(bf16[768,2048]{1,0:T(8,128)(2,1)} %get-tuple-element.27) | copy-start | bytes 9437188

commit v4 on v3

--- a/solution.py
+++ b/solution.py
@@ -226,41 +226,38 @@
     for w in loads:
         w.wait()
 
-    def fetch(n, s):
+    @pl.loop(0, NJ)
+    def _(n):
         j = source(n)
         landed(xr.at[j], p2r.at[j])
         landed(gr.at[j], q2r.at[j])
-        pltpu.make_async_copy(xr.at[j], stx.at[s], xsem.at[s]).start()
-        pltpu.make_async_copy(gr.at[j], stg.at[s], gsem.at[s]).start()
-
-    @pl.loop(0, NJ)
-    def _(n):
-        s = lax.rem(n, 2)
+        x_in = pltpu.make_async_copy(xr.at[j], stx, xsem.at[0])
+        g_in = pltpu.make_async_copy(gr.at[j], stg, gsem.at[0])
+        x_in.start()
+        g_in.start()
+        x_in.wait()
+        g_in.wait()
+        xb = stx[...].reshape(2 * T, D)
+        gate_pre = dot(xb, wg[...])
+        up_pre = dot(xb, wu[...])
+        hgrad = dot(stg[...].reshape(2 * T, D), wd[...], 1, 1)
+        sigma = jax.nn.sigmoid(gate_pre)
+        act = gate_pre * sigma
+        slot_n = lax.rem(n, 2)
 
         @pl.when(n >= 2)
         def _():
-            landed(ost.at[s], osem.at[s])
-
-        fetch(n, s)
-        landed(stx.at[s], xsem.at[s])
-        landed(stg.at[s], gsem.at[s])
-        xb = stx[s].reshape(2 * T, D)
-        gb = stg[s].reshape(2 * T, D)
-        gate_pre = dot(xb, wg[...])
-        up_pre = dot(xb, wu[...])
-        hgrad = dot(gb, wd[...], 1, 1)
-        sigma = jax.nn.sigmoid(gate_pre)
-        act = gate_pre * sigma
-        ost[s, 0] = (act * up_pre).astype(BF)
-        ost[s, 1] = (hgrad * up_pre * sigma * (1.0 + gate_pre * (1.0 - sigma))).astype(BF)
-        ost[s, 2] = (hgrad * act).astype(BF)
-        for v, out in enumerate((hid_o, gg_o, ug_o)):
-            pltpu.make_async_copy(ost.at[s, v], out.at[source(n)], osem.at[s]).start()
-
+            landed(ost.at[slot_n], osem.at[slot_n])
+
+        ost[slot_n] = (act * up_pre).astype(BF)
+        pltpu.make_async_copy(ost.at[slot_n], hid_o.at[j], osem.at[slot_n]).start()
+        gg_o[j] = (hgrad * up_pre * sigma * (1.0 + gate_pre * (1.0 - sigma))).astype(BF)
+        ug_o[j] = (hgrad * act).astype(BF)
+
+    for n in range(2):
+        landed(ost.at[n], osem.at[n])
     pos_o[...] = pos_r[...]
     rank_o[...] = rank_r[...]
-    for s in range(2):
-        landed(ost.at[s], osem.at[s])
     for k in range(1, NJ):
         to = lax.rem(own + k, NJ)
         landed(rank_s.at[to], ms.at[k])
@@ -277,24 +274,22 @@
 
 
 def combine_kernel(
-    c_ref, pos_ref, rank_ref, xr, gr, hid_hbm, gg_hbm, ug_hbm, wg_hbm, wu_hbm,
+    c_ref, pos_ref, rank_ref, xr, gr, hid_hbm, gg, ug, wg_hbm, wu_hbm,
     gin_o, dg_o, du_o, dd_o,
-    hid, gg, ug, wg, wu, dxp, dxq, rrp, rrq, part, rrz, s2, rr2, xcol, gcol, ogu, od,
-    lsem, p1s, p1r, p2s, p2r, t1s, t1r, t2s, t2r, xsem, gsem, gusem, dsem,
+    hid, wg, wu, dxp, dxq, rrp, rrq, part, rrz, s2, rr2, xcol, gcol,
+    wsem, p1s, p1r, p2s, p2r, t1s, t1r, t2s, t2r, xsem, gsem,
 ):
     grp, own = lax.axis_index("group"), lax.axis_index("expert")
     barrier = enter(grp, own)
     loads = [
-        pltpu.make_async_copy(src, dst, lsem.at[n])
-        for n, (src, dst) in enumerate(
-            ((gg_hbm, gg), (ug_hbm, ug), (wg_hbm, wg), (wu_hbm, wu), (hid_hbm, hid))
-        )
+        pltpu.make_async_copy(wg_hbm, wg, wsem.at[0]),
+        pltpu.make_async_copy(wu_hbm, wu, wsem.at[1]),
+        pltpu.make_async_copy(hid_hbm, hid, wsem.at[2]),
     ]
     for w in loads:
         w.start()
-    for w in loads[:4]:
+    for w in loads[:2]:
         w.wait()
-    pl.semaphore_wait(barrier, NG + NJ - 2)
 
     def slot_rows(a):
         return pl.ds(pl.multiple_of(a * CAP, CAP), CAP)
@@ -304,19 +299,10 @@
             dot(ggb, wg[c : c + 512, :], 1, 1) + dot(ugb, wu[c : c + 512, :], 1, 1)
         ).astype(BF)
 
-    @pl.loop(0, NJ)
-    def _(n):
+    def make_rows(n):
         j = lax.rem(own + 4 + n, NJ)
         for c in range(0, DP, 512):
             dxp[j, :, c : c + 512] = input_rows(gg[j], ug[j], c)
-        for d in OUTWARD:
-            a = group_to(grp, d)
-            send(dxp.at[j, slot_rows(a)], rrp.at[j, slot_rows(grp)],
-                 p1s.at[j], p1r.at[j], (a, own))
-        pltpu.make_async_copy(
-            dxp.at[j, slot_rows(grp)], rrp.at[j, slot_rows(grp)], p1r.at[j]
-        ).start()
-
         tops = [group_to(grp, 2 * n + h) for h in range(2)]
         ats = [slot_rows(a) for a in tops]
         ggb = jnp.concatenate([gg[q, at, :] for at in ats for q in range(NJ)], axis=0)
@@ -325,7 +311,18 @@
             rows = input_rows(ggb, ugb, c)
             for h in range(2):
                 dxq[tops[h], :, c - DP : c - DP + 512] = rows[h * T : (h + 1) * T, :]
-        for a in tops:
+
+    def send_rows(n):
+        j = lax.rem(own + 4 + n, NJ)
+        for d in OUTWARD:
+            a = group_to(grp, d)
+            send(dxp.at[j, slot_rows(a)], rrp.at[j, slot_rows(grp)],
+                 p1s.at[j], p1r.at[j], (a, own))
+        pltpu.make_async_copy(
+            dxp.at[j, slot_rows(grp)], rrp.at[j, slot_rows(grp)], p1r.at[j]
+        ).start()
+        for h in range(2):
+            a = group_to(grp, 2 * n + h)
             for k in range(1, NJ):
                 to = lax.rem(own + k, NJ)
                 send(dxq.at[a, slot_rows(to)], rrq.at[a, slot_rows(own)],
@@ -334,7 +331,16 @@
                 dxq.at[a, slot_rows(own)], rrq.at[a, slot_rows(own)], t1r.at[a]
             ).start()
 
-    loads[4].wait()
+    make_rows(0)
+    pl.semaphore_wait(barrier, NG + NJ - 2)
+    send_rows(0)
+
+    @pl.loop(1, NJ)
+    def _(n):
+        make_rows(n)
+        send_rows(n)
+
+    loads[2].wait()
     spot = iota((PG, T), 0)
 
     def fetch(c, s):
@@ -348,11 +354,6 @@
     def _(i):
         s = lax.rem(i, 2)
 
-        @pl.when(i >= 2)
-        def _():
-            landed(ogu.at[s], gusem.at[s])
-            landed(od.at[s], dsem.at[s])
-
         @pl.when(i + 1 < NJ)
         def _():
             fetch(i + 1, 1 - s)
@@ -361,12 +362,9 @@
         landed(gcol.at[s], gsem.at[s])
         at = pl.ds(pl.multiple_of(i * 256, 256), 256)
         xc = xcol[s]
-        ogu[s, 0] = dot(xc, gg[...].reshape(ROWS, FF), 0, 0).astype(BF)
-        ogu[s, 1] = dot(xc, ug[...].reshape(ROWS, FF), 0, 0).astype(BF)
-        od[s] = dot(hid[...].reshape(ROWS, FF), gcol[s], 0, 0).astype(BF)
-        pltpu.make_async_copy(ogu.at[s, 0], dg_o.at[at, :], gusem.at[s]).start()
-        pltpu.make_async_copy(ogu.at[s, 1], du_o.at[at, :], gusem.at[s]).start()
-        pltpu.make_async_copy(od.at[s], dd_o.at[:, at], dsem.at[s]).start()
+        dg_o[at, :] = dot(xc, gg[...].reshape(ROWS, FF), 0, 0).astype(BF)
+        du_o[at, :] = dot(xc, ug[...].reshape(ROWS, FF), 0, 0).astype(BF)
+        dd_o[:, at] = dot(hid[...].reshape(ROWS, FF), gcol[s], 0, 0).astype(BF)
 
         j = lax.rem(own + 4 + i, NJ)
         landed(rrp.at[j], p1r.at[j])
@@ -414,9 +412,6 @@
         rows = rr2[:, :, c : c + 512].reshape(NG * PG, 512)
         gin_o[:, DP + c : DP + c + 512] = dot(c_ref[...], rows, 0, 0).astype(BF)
 
-    for s in range(2):
-        landed(ogu.at[s], gusem.at[s])
-        landed(od.at[s], dsem.at[s])
     for a in range(NG):
         landed(dxq.at[a, pl.ds(0, (NJ - 1) * CAP)], t1s.at[a])
     for j in range(NJ):
@@ -440,42 +435,44 @@
         name="dispatch",
         out_shape=(
             shape((NJ, NG, CAP, D), BF), shape((NJ, NG, CAP, D), BF),
-            shape((NJ, 2 * T, FF), BF), shape((NJ, 2 * T, FF), BF), shape((NJ, 2 * T, FF), BF),
-            shape((NG * PG, T), BF), shape((NG, 8, 128), I32), shape((NJ, NG, T), I32),
+            shape((NJ, 2 * T, FF), BF), pltpu.VMEM((NJ, 2 * T, FF), BF),
+            pltpu.VMEM((NJ, 2 * T, FF), BF),
+            pltpu.VMEM((NG * PG, T), BF), pltpu.VMEM((NG, 8, 128), I32),
+            pltpu.VMEM((NJ, NG, T), I32),
         ),
         in_specs=[vm, vm, hbm, vm, hbm, hbm, hbm],
-        out_specs=(hbm, hbm, hbm, hbm, hbm, vm, vm, vm),
+        out_specs=(hbm, hbm, hbm) + (vm,) * 5,
         scratch_shapes=[
             pltpu.VMEM((NJ, T, D), BF),
             pltpu.VMEM((NJ, NG, CAP, D), BF),
             pltpu.VMEM((NG, PG, D), BF),
             pltpu.VMEM((NG, PG, D), BF),
             pltpu.VMEM((NG, NJ * CAP, D), BF),
-            pltpu.VMEM((2, NG, CAP, D), BF),
-            pltpu.VMEM((2, NG, CAP, D), BF),
+            pltpu.VMEM((NG, CAP, D), BF),
+            pltpu.VMEM((NG, CAP, D), BF),
             pltpu.VMEM((D, FF), BF), pltpu.VMEM((D, FF), BF), pltpu.VMEM((FF, D), BF),
-            pltpu.VMEM((2, 3, 2 * T, FF), BF),
+            pltpu.VMEM((2, 2 * T, FF), BF),
             pltpu.VMEM((NJ, NG, T), I32), pltpu.VMEM((NJ, NG, T), I32),
             pltpu.VMEM((NG, 8, 128), I32), pltpu.VMEM((NG, 8, 128), I32),
             pltpu.VMEM((E, T), I32), pltpu.VMEM((E, T), F32),
             sem((7,)), sem((NJ,)), sem((NJ,)), sem((NJ,)),
             sem((NG,)), sem((NG,)), sem((NG,)), sem((NG,)), sem((NG,)), sem((NG,)),
-            sem((NG,)), sem((NG,)), sem((3,)), sem((2,)), sem((2,)), sem((2,)),
+            sem((NG,)), sem((NG,)), sem((3,)), sem((1,)), sem((1,)), sem((2,)),
         ],
         compiler_params=pltpu.CompilerParams(
-            collective_id=0, has_side_effects=True, vmem_limit_bytes=VMEM_LIMIT
+            collective_id=0, has_side_effects=True, vmem_limit_bytes=48 << 20
         ),
     )(expert_ids.T, gate_weights.T, tokens_in, out_grad, wg, wu, wd)
     grad_in, d_gate, d_up, d_down = pl.pallas_call(
         combine_kernel,
         name="combine",
         out_shape=(
-            shape((T, D), BF), shape((D, FF), BF), shape((D, FF), BF), shape((FF, D), BF),
+            pltpu.VMEM((T, D), BF), pltpu.VMEM((D, FF), BF),
+            pltpu.VMEM((D, FF), BF), pltpu.VMEM((FF, D), BF),
         ),
-        in_specs=[vm, vm, vm] + [hbm] * 7,
-        out_specs=(vm, hbm, hbm, hbm),
+        in_specs=[vm, vm, vm, hbm, hbm, hbm, vm, vm, hbm, hbm],
+        out_specs=(vm, vm, vm, vm),
         scratch_shapes=[
-            pltpu.VMEM((NJ, 2 * T, FF), BF), pltpu.VMEM((NJ, 2 * T, FF), BF),
             pltpu.VMEM((NJ, 2 * T, FF), BF),
             pltpu.VMEM((D, FF), BF), pltpu.VMEM((D, FF), BF),
             pltpu.VMEM((NJ, 2 * T, DP), BF),
@@ -487,15 +484,16 @@
             pltpu.VMEM((NG, PG, D - DP), BF),
             pltpu.VMEM((NG, PG, D - DP), BF),
             pltpu.VMEM((2, ROWS, 256), BF), pltpu.VMEM((2, ROWS, 256), BF),
-            pltpu.VMEM((2, 2, 256, FF), BF), pltpu.VMEM((2, FF, 256), BF),
-            sem((5,)), sem((NJ,)), sem((NJ,)), sem((NJ,)), sem((NJ,)),
+            sem((3,)), sem((NJ,)), sem((NJ,)), sem((NJ,)), sem((NJ,)),
             sem((NG,)), sem((NG,)), sem((NG,)), sem((NG,)),
-            sem((2,)), sem((2,)), sem((2,)), sem((2,)),
+            sem((2,)), sem((2,)),
         ],
         compiler_params=pltpu.CompilerParams(
-            collective_id=1, has_side_effects=True, vmem_limit_bytes=VMEM_LIMIT
+            collective_id=1, has_side_effects=True, vmem_limit_bytes=42 << 20
         ),
-    )(hots, pos, rank, xr.reshape(ROWS, D), gr.reshape(ROWS, D), hid, gg, ug, wg, wu)
+    )(*[pltpu.with_memory_space_constraint(v, pltpu.VMEM) for v in (hots, pos, rank)], xr.reshape(ROWS, D), gr.reshape(ROWS, D), hid,
+      *[pltpu.with_memory_space_constraint(v, pltpu.VMEM) for v in (gg, ug)],
+      wg, wu)
     return grad_in, d_gate[None], d_up[None], d_down[None]
 
 

time: 250 us -> 240 us (0.960)
  local copies, waits for them, and re-layouts: 10.5 us -> 5.79 us
  Pallas kernels: 236 us -> 232 us
    unnamed x8 -> x4, local copies, waits for them, and re-layouts: 10.5 us -> 5.79 us
    pallas_call x1, Pallas kernels: 82 us -> 79.5 us  [body(): pl.pallas_call(combine_kernel, name='combine', out_shape=(pltpu.VMEM((T,...]
where the time goes in v4:
time: 240 us; the launch traced here: 239 us
  Pallas kernels  232 us (97%)
  local copies, waits for them, and re-layouts  5.79 us (2%)
    pallas_call x1, Pallas kernels, body(): pl.pallas_call(dispatch_kernel, name='dispatch', out_shape=(shape((NJ, NG...  153 us
    pallas_call x1, Pallas kernels, body(): pl.pallas_call(combine_kernel, name='combine', out_shape=(pltpu.VMEM((T,...  79.5 us
    unnamed x4, local copies, waits for them, and re-layouts  5.79 us

profile of v4, /device:TPU:9, one launch (start us, length us, event | category | flops | bytes accessed | tf_op | source)
XLA Modules:
  0.0 238.7 jit_solution(2442600193039429261)
XLA Ops:
  0.6 152.8 %dispatch.1 = (bf16[8,16,16,2048]{3,2,1,0:T(8,128)(2,1)}, bf16[8,16,16,2048]{3,2,1,0:T(8,128)(2,1)}, bf16[8,256,768]{2,1,0:T(8,128)(2,1)}, bf16[8,256,768]{2,1,0...) custom-call(s32[8,128]{1,0:T(8,128)} %bitcast.20, ...), custom_call_target="tpu_custom_call" | custom-call | tf_op jit(solution)/shard_map/dispatch/pallas_call | solution.py:433
  153.4 79.5 %combine.1 = (bf16[128,2048]{1,0:T(8,128)(2,1)S(1)}, bf16[2048,768]{1,0:T(8,128)(2,1)S(1)}, bf16[2048,768]{1,0:T(8,128)(2,1)S(1)}, bf16[768,2048]{1,0:T(8,128)(2,1)S(1)}) custom-call(bf16[1024,128]{1,0:T(8,128)(2,1)S(1)} %get-tuple-element.16.c_ref, s32[16,8,128]{2,1,0:T(8,128)S(1)} %get-tuple-element.17.pos_ref, ...), custom_call_target="tpu_custom_call" | custom-call | tf_op jit(solution)/shard_map/combine/pallas_call | solution.py:466
  232.9 0.8 copy.15
  233.7 1.7 copy.16
  235.4 1.7 copy.17
  237.0 1.7 copy.18

commit v5 on v4

--- a/solution.py
+++ b/solution.py
@@ -422,6 +422,22 @@
     for d in range(1, NG):
         a = group_to(grp, d)
         landed(s2.at[a], t2s.at[a])
+
+
+def store_kernel(*refs):
+    sems = refs[8]
+    copies = []
+    for n in range(4):
+        size = refs[n].shape[0] // 4
+        for q in range(4):
+            at = pl.ds(q * size, size)
+            copies.append(
+                pltpu.make_async_copy(refs[n].at[at], refs[4 + n].at[at], sems.at[n, q])
+            )
+    for copy in copies:
+        copy.start()
+    for copy in copies:
+        copy.wait()
 
 
 def body(tokens_in, out_grad, expert_ids, gate_weights, w_gate, w_up, w_down):
@@ -494,6 +510,16 @@
     )(*[pltpu.with_memory_space_constraint(v, pltpu.VMEM) for v in (hots, pos, rank)], xr.reshape(ROWS, D), gr.reshape(ROWS, D), hid,
       *[pltpu.with_memory_space_constraint(v, pltpu.VMEM) for v in (gg, ug)],
       wg, wu)
+    outs = [pltpu.with_memory_space_constraint(v, pltpu.VMEM) for v in (grad_in, d_gate, d_up, d_down)]
+    grad_in, d_gate, d_up, d_down = pl.pallas_call(
+        store_kernel,
+        name="store",
+        out_shape=tuple(shape(v.shape, BF) for v in outs),
+        in_specs=[vm] * 4,
+        out_specs=(hbm,) * 4,
+        scratch_shapes=[sem((4, 4))],
+        compiler_params=pltpu.CompilerParams(vmem_limit_bytes=1 << 20),
+    )(*outs)
     return grad_in, d_gate[None], d_up[None], d_down[None]
 
 

time: 240 us -> 238 us (level)
  local copies, waits for them, and re-layouts: 5.79 us -> 0 us
  Pallas kernels: 232 us -> 236 us
    unnamed x4 -> x0, local copies, waits for them, and re-layouts: 5.79 us -> none
    pallas_call x0 -> x1, Pallas kernels: none -> 3.91 us  [body(): pl.pallas_call(store_kernel, name='store', out_shape=tuple((shape(v.shape...]
where the time goes in v5:
time: 238 us; the launch traced here: 237 us
  Pallas kernels  236 us (99%)
    pallas_call x1, Pallas kernels, body(): pl.pallas_call(dispatch_kernel, name='dispatch', out_shape=(shape((NJ, NG...  153 us
    pallas_call x1, Pallas kernels, body(): pl.pallas_call(combine_kernel, name='combine', out_shape=(pltpu.VMEM((T,...  79.5 us

profile of v5, /device:TPU:9, one launch (start us, length us, event | category | flops | bytes accessed | tf_op | source)
XLA Modules:
  0.0 237.0 jit_solution(7892069877061964488)
XLA Ops:
  0.6 152.8 %dispatch.1 = (bf16[8,16,16,2048]{3,2,1,0:T(8,128)(2,1)}, bf16[8,16,16,2048]{3,2,1,0:T(8,128)(2,1)}, bf16[8,256,768]{2,1,0:T(8,128)(2,1)}, bf16[8,256,768]{2,1,0...) custom-call(s32[8,128]{1,0:T(8,128)} %bitcast.17, ...), custom_call_target="tpu_custom_call" | custom-call | tf_op jit(solution)/shard_map/dispatch/pallas_call | solution.py:449
  153.4 79.5 %combine.1 = (bf16[128,2048]{1,0:T(8,128)(2,1)S(1)}, bf16[2048,768]{1,0:T(8,128)(2,1)S(1)}, bf16[2048,768]{1,0:T(8,128)(2,1)S(1)}, bf16[768,2048]{1,0:T(8,128)(2,1)S(1)}) custom-call(bf16[1024,128]{1,0:T(8,128)(2,1)S(1)} %get-tuple-element.20.c_ref, s32[16,8,128]{2,1,0:T(8,128)S(1)} %get-tuple-element.21.pos_ref, ...), custom_call_target="tpu_custom_call" | custom-call | tf_op jit(solution)/shard_map/combine/pallas_call | solution.py:482
  232.9 3.9 %store.1 = (bf16[128,2048]{1,0:T(8,128)(2,1)}, bf16[2048,768]{1,0:T(8,128)(2,1)}, bf16[2048,768]{1,0:T(8,128)(2,1)}, bf16[768,2048]{1,0:T(8,128)(2,1)}) custom-call(bf16[128,2048]{1,0:T(8,128)(2,1)S(1)} %get-tuple-element.28.refs_0_, bf16[2048,768]{1,0:T(8,128)(2,1)S(1)} %get-tuple-element.29.refs_1_, bf16[2048,768]{1,0:T(8,128)(2,1)S(1)} %get-tuple-element.30.refs_2_, ...), custom_call_target="tpu_custom_call" | custom-call | tf_op jit(solution)/shard_map/store/pallas_call | solution.py:514

commit v6 on v4

--- a/solution.py
+++ b/solution.py
@@ -274,9 +274,9 @@
 
 
 def combine_kernel(
-    c_ref, pos_ref, rank_ref, xr, gr, hid_hbm, gg, ug, wg_hbm, wu_hbm,
-    gin_o, dg_o, du_o, dd_o,
-    hid, wg, wu, dxp, dxq, rrp, rrq, part, rrz, s2, rr2, xcol, gcol,
+    pos_ref, rank_ref, xr, gr, hid_hbm, gg, ug, wg_hbm, wu_hbm,
+    dg_o, du_o, dd_o, rrz, rr2,
+    hid, wg, wu, dxp, dxq, rrp, rrq, part, s2, xcol, gcol,
     wsem, p1s, p1r, p2s, p2r, t1s, t1r, t2s, t2r, xsem, gsem,
 ):
     grp, own = lax.axis_index("group"), lax.axis_index("expert")
@@ -401,17 +401,8 @@
 
     for j in range(NJ):
         landed(rrz.at[j], p2r.at[j])
-    for c in range(0, DP, 512):
-        total = rrz[0, :, c : c + 512].astype(F32)
-        for j in range(1, NJ):
-            total = total + rrz[j, :, c : c + 512].astype(F32)
-        gin_o[:, c : c + 512] = total.astype(BF)
     for a in range(NG):
         landed(rr2.at[a], t2r.at[a])
-    for c in range(0, D - DP, 512):
-        rows = rr2[:, :, c : c + 512].reshape(NG * PG, 512)
-        gin_o[:, DP + c : DP + c + 512] = dot(c_ref[...], rows, 0, 0).astype(BF)
-
     for a in range(NG):
         landed(dxq.at[a, pl.ds(0, (NJ - 1) * CAP)], t1s.at[a])
     for j in range(NJ):
@@ -422,6 +413,30 @@
     for d in range(1, NG):
         a = group_to(grp, d)
         landed(s2.at[a], t2s.at[a])
+
+
+def store_kernel(c_ref, rrz, rr2, dg, du, dd, gin_o, dg_o, du_o, dd_o, gin, sems, gsem):
+    copies = []
+    for n, (src, dst) in enumerate(((dg, dg_o), (du, du_o), (dd, dd_o))):
+        size = src.shape[0] // 4
+        for q in range(4):
+            at = pl.ds(q * size, size)
+            copies.append(pltpu.make_async_copy(src.at[at], dst.at[at], sems.at[n, q]))
+    for copy in copies:
+        copy.start()
+    for c in range(0, DP, 512):
+        total = rrz[0, :, c : c + 512].astype(F32)
+        for j in range(1, NJ):
+            total = total + rrz[j, :, c : c + 512].astype(F32)
+        gin[:, c : c + 512] = total.astype(BF)
+    for c in range(0, D - DP, 512):
+        rows = rr2[:, :, c : c + 512].reshape(NG * PG, 512)
+        gin[:, DP + c : DP + c + 512] = dot(c_ref[...], rows, 0, 0).astype(BF)
+    last = pltpu.make_async_copy(gin, gin_o, gsem.at[0])
+    last.start()
+    for copy in copies:
+        copy.wait()
+    last.wait()
 
 
 def body(tokens_in, out_grad, expert_ids, gate_weights, w_gate, w_up, w_down):
@@ -463,15 +478,15 @@
             collective_id=0, has_side_effects=True, vmem_limit_bytes=48 << 20
         ),
     )(expert_ids.T, gate_weights.T, tokens_in, out_grad, wg, wu, wd)
-    grad_in, d_gate, d_up, d_down = pl.pallas_call(
+    d_gate, d_up, d_down, sums, rows = pl.pallas_call(
         combine_kernel,
         name="combine",
         out_shape=(
-            pltpu.VMEM((T, D), BF), pltpu.VMEM((D, FF), BF),
-            pltpu.VMEM((D, FF), BF), pltpu.VMEM((FF, D), BF),
+            pltpu.VMEM((D, FF), BF), pltpu.VMEM((D, FF), BF), pltpu.VMEM((FF, D), BF),
+            pltpu.VMEM((NJ, T, DP), BF), pltpu.VMEM((NG, PG, D - DP), BF),
         ),
-        in_specs=[vm, vm, vm, hbm, hbm, hbm, vm, vm, hbm, hbm],
-        out_specs=(vm, vm, vm, vm),
+        in_specs=[vm, vm, hbm, hbm, hbm, vm, vm, hbm, hbm],
+        out_specs=(vm,) * 5,
         scratch_shapes=[
             pltpu.VMEM((NJ, 2 * T, FF), BF),
             pltpu.VMEM((D, FF), BF), pltpu.VMEM((D, FF), BF),
@@ -480,8 +495,6 @@
             pltpu.VMEM((NJ, 2 * T, DP), BF),
             pltpu.VMEM((NG, T, D - DP), BF),
             pltpu.VMEM((NJ, T, DP), BF),
-            pltpu.VMEM((NJ, T, DP), BF),
-            pltpu.VMEM((NG, PG, D - DP), BF),
             pltpu.VMEM((NG, PG, D - DP), BF),
             pltpu.VMEM((2, ROWS, 256), BF), pltpu.VMEM((2, ROWS, 256), BF),
             sem((3,)), sem((NJ,)), sem((NJ,)), sem((NJ,)), sem((NJ,)),
@@ -489,11 +502,25 @@
             sem((2,)), sem((2,)),
         ],
         compiler_params=pltpu.CompilerParams(
-            collective_id=1, has_side_effects=True, vmem_limit_bytes=42 << 20
+            collective_id=1, has_side_effects=True, vmem_limit_bytes=38 << 20
         ),
-    )(*[pltpu.with_memory_space_constraint(v, pltpu.VMEM) for v in (hots, pos, rank)], xr.reshape(ROWS, D), gr.reshape(ROWS, D), hid,
+    )(*[pltpu.with_memory_space_constraint(v, pltpu.VMEM) for v in (pos, rank)], xr.reshape(ROWS, D), gr.reshape(ROWS, D), hid,
       *[pltpu.with_memory_space_constraint(v, pltpu.VMEM) for v in (gg, ug)],
       wg, wu)
+    grad_in, d_gate, d_up, d_down = pl.pallas_call(
+        store_kernel,
+        name="store",
+        out_shape=(
+            shape((T, D), BF), shape((D, FF), BF), shape((D, FF), BF), shape((FF, D), BF),
+        ),
+        in_specs=[vm] * 6,
+        out_specs=(hbm,) * 4,
+        scratch_shapes=[pltpu.VMEM((T, D), BF), sem((3, 4)), sem((1,))],
+        compiler_params=pltpu.CompilerParams(vmem_limit_bytes=4 << 20),
+    )(*[
+        pltpu.with_memory_space_constraint(v, pltpu.VMEM)
+        for v in (hots, sums, rows, d_gate, d_up, d_down)
+    ])
     return grad_in, d_gate[None], d_up[None], d_down[None]
 
 

time: 240 us -> 238 us (level)
  local copies, waits for them, and re-layouts: 5.79 us -> 0 us
  Pallas kernels: 232 us -> 236 us
    unnamed x4 -> x0, local copies, waits for them, and re-layouts: 5.79 us -> none
    pallas_call x1 -> x2, Pallas kernels: 79.5 us -> 82.9 us  [the longest x1 79 us: body(): pl.pallas_call(combine_kernel, name='combine', out_shape=(pltpu.VMEM((D,...]
where the time goes in v6:
time: 238 us; the launch traced here: 237 us
  Pallas kernels  236 us (99%)
    pallas_call x1, Pallas kernels, body(): pl.pallas_call(dispatch_kernel, name='dispatch', out_shape=(shape((NJ, NG...  153 us
    pallas_call x1, Pallas kernels, body(): pl.pallas_call(combine_kernel, name='combine', out_shape=(pltpu.VMEM((D,...  79 us

profile of v6, /device:TPU:9, one launch (start us, length us, event | category | flops | bytes accessed | tf_op | source)
XLA Modules:
  0.0 236.5 jit_solution(3670011176529643195)
XLA Ops:
  0.6 152.8 %dispatch.1 = (bf16[8,16,16,2048]{3,2,1,0:T(8,128)(2,1)}, bf16[8,16,16,2048]{3,2,1,0:T(8,128)(2,1)}, bf16[8,256,768]{2,1,0:T(8,128)(2,1)}, bf16[8,256,768]{2,1,0...) custom-call(s32[8,128]{1,0:T(8,128)} %bitcast.17, ...), custom_call_target="tpu_custom_call" | custom-call | tf_op jit(solution)/shard_map/dispatch/pallas_call | solution.py:448
  153.4 79.0 %combine.1 = (bf16[2048,768]{1,0:T(8,128)(2,1)S(1)}, bf16[2048,768]{1,0:T(8,128)(2,1)S(1)}, bf16[768,2048]{1,0:T(8,128)(2,1)S(1)}, bf16[8,128,1024]{2,1,0:T(8,128)(2,1)S(1)}, bf16[16,64,1024]{2,1,0:T(8,128)(2,1)S(1)}) custom-call(s32[16,8,128]{2,1,0:T(8,128)S(1)} %get-tuple-element.22.pos_ref, s32[8,16,128]{2,1,0:T(8,128)S(1)} %get-tuple-element.23.rank_ref, ...), custom_call_target="tpu_custom_call" | custom-call | tf_op jit(solution)/shard_map/combine/pallas_call | solution.py:481
  232.4 3.9 %store.1 = (bf16[128,2048]{1,0:T(8,128)(2,1)}, bf16[2048,768]{1,0:T(8,128)(2,1)}, bf16[2048,768]{1,0:T(8,128)(2,1)}, bf16[768,2048]{1,0:T(8,128)(2,1)}) custom-call(bf16[1024,128]{1,0:T(8,128)(2,1)S(1)} %get-tuple-element.21.c_ref, bf16[8,128,1024]{2,1,0:T(8,128)(2,1)S(1)} %get-tuple-element.29.rrz, bf16[16,64,1024]{2,1,0:T(8,128)(2,1)S(1)} %get-tuple-element.30.rr2, ...), custom_call_target="tpu_custom_call" | custom-call | tf_op jit(solution)/shard_map/store/pallas_call | solution.py:510
